TPU v7x, 256 devices: a whole 4x4x8 slice. The times are simulated.
256 devices in a mesh: row: 4 (over x), col: 64 (over y, z, core).
Axes of the slice: x: 4, y: 4, z: 8, core: 2. Of those that a mesh axis runs over, the one named last changes fastest.
Arguments:
- child_rhs: bfloat16 [12288, 128, 128], P(('row', 'col')), may hold values from -6 to 6
- parent_rhs: bfloat16 [64, 128, 128], P('col'), may hold values from -6 to 6
- child_lower_inv: bfloat16 [12288, 128, 128], P(('row', 'col')), may hold values from -0.5 to 0.5
- child_lower_off: bfloat16 [12288, 128, 128], P(('row', 'col')), may hold values from -0.125 to 0.125
- child_upper_inv: bfloat16 [12288, 128, 128], P(('row', 'col')), may hold values from -0.5 to 0.5
- child_upper_off: bfloat16 [12288, 128, 128], P(('row', 'col')), may hold values from -0.25 to 0.25
- parent_lower_inv: bfloat16 [64, 128, 128], P('col'), may hold values from -0.5 to 0.5
- parent_upper_inv: bfloat16 [64, 128, 128], P('col'), may hold values from -0.5 to 0.5
- parent_of: int32 [12288], P(('row', 'col')), may hold values from 0 to 63
Outputs:
- child_solution: bfloat16 [12288, 128, 128], P(('row', 'col'))
- parent_solution: bfloat16 [64, 128, 128], P('col')
Inputs may be any that keep to these rules, and one draw needn't show every extreme that they name: `parent_of`: each lower-level supernode names one upper-level parent.
All inputs are finite; a program needn't handle non-finite values.
Results may differ from a plain program's by a relative error of at most 0.0095.
Values may be sent and summed in bfloat16 or wider, within the bound.
A program may use at most 64 MiB of HBM per device.

v0:
```python
import jax
import jax.numpy as jnp
from jax import lax
from jax.sharding import Mesh
from jax.sharding import PartitionSpec as P

COL = ("col_0", "col_1", "col_2")
ROW_COL = ("row", "col_0", "col_1", "col_2")


def split_up(x, dim, count):
    dims = x.shape
    pieces = x.reshape(*dims[:dim], count, dims[dim] // count, *dims[dim + 1 :])
    return jnp.moveaxis(pieces, dim, 0)


def summed_on_arrival(x, axis, dim):
    pieces = split_up(x, dim, lax.axis_size(axis))
    arrived = lax.all_to_all(pieces, axis, split_axis=0, concat_axis=0, tiled=True)
    return arrived.sum(axis=0)


def summed_rows(x, axes, dim):
    far, near = axes
    own = summed_on_arrival(split_up(x, dim, lax.axis_size(far)), near, dim + 1)
    return jnp.sum(lax.all_to_all(own, far, 0, 0, tiled=True), axis=0)


def from_everyone(x, axis):
    count = lax.axis_size(axis)
    return lax.all_to_all(jnp.broadcast_to(x[None], (count, *x.shape)), axis, 0, 0, tiled=True)


def of_everyone(x, axis):
    everything = from_everyone(x, axis)
    return jnp.sum(everything, axis=0)


def laid_out(pieces, dim):
    pieces = jnp.moveaxis(pieces, 0, dim)
    dims = pieces.shape
    return pieces.reshape(*dims[:dim], dims[dim] * dims[dim + 1], *dims[dim + 2 :])


def whole_of(x, axes, dim):
    far, near = axes
    initial = from_everyone(x, far)
    pieces = jnp.swapaxes(from_everyone(initial, near), 0, 1)
    return laid_out(pieces.reshape(-1, *x.shape), dim)


def product(mats, vals):
    return jnp.einsum("cij,cjr->cir", mats, vals, preferred_element_type=jnp.float32)


def on_device(
    child_rhs,
    parent_rhs,
    child_lower_inv,
    child_lower_off,
    child_upper_inv,
    child_upper_off,
    parent_lower_inv,
    parent_upper_inv,
    parent_of,
):
    per_col = parent_rhs.shape[0]
    n_col = lax.axis_size(COL)
    parents = per_col * n_col
    child_forward = product(child_lower_inv, child_rhs).astype(jnp.bfloat16)
    contrib = product(child_lower_off, child_forward)
    labels = jnp.arange(parents, dtype=jnp.int32)
    onehot = (parent_of[:, None] == labels[None, :]).astype(jnp.float32)
    partial_sum = jnp.einsum("cp,cwr->pwr", onehot, contrib, precision=lax.Precision.HIGHEST)
    mine = summed_rows(partial_sum, (("col_0", "col_1"), "col_2"), 0)
    update = of_everyone(mine, "row")
    parent_residual = (parent_rhs.astype(jnp.float32) - update).astype(jnp.bfloat16)
    parent_forward = product(parent_lower_inv, parent_residual).astype(jnp.bfloat16)
    parent_solution = product(parent_upper_inv, parent_forward).astype(jnp.bfloat16)
    gathered = whole_of(parent_solution, (("col_0", "col_1"), "col_2"), 0)
    picked = jnp.take(gathered, parent_of, axis=0)
    child_residual = (child_forward.astype(jnp.float32) - product(child_upper_off, picked)).astype(
        jnp.bfloat16
    )
    child_solution = product(child_upper_inv, child_residual).astype(jnp.bfloat16)
    return (child_solution, parent_solution)


def solution(mesh):
    finer = Mesh(
        mesh.devices.reshape(mesh.shape["row"], 4, 8, 2), ("row", "col_0", "col_1", "col_2")
    )
    return jax.shard_map(
        on_device,
        mesh=finer,
        in_specs=(
            P(ROW_COL, None, None),
            P(COL, None, None),
            P(ROW_COL, None, None),
            P(ROW_COL, None, None),
            P(ROW_COL, None, None),
            P(ROW_COL, None, None),
            P(COL, None, None),
            P(COL, None, None),
            P(ROW_COL),
        ),
        out_specs=(P(ROW_COL, None, None), P(COL, None, None)),
        check_vma=False,
    )
```

profile of v0, /device:TPU:1, one launch (start us, length us, event | category | flops | bytes accessed | tf_op | source)
XLA Modules:
  0.0 161.2 jit_solution(10479975530927697110)
XLA Ops:
  0.6 0.0 copy-start
  0.6 0.0 copy-start.1
  0.7 1.4 copy-done
  2.0 2.0 %convolution_convert_fusion.1 = bf16[48,128,128]{2,1,0:T(8,128)(2,1)S(1)} fusion(bf16[48,128,128]{2,1,0:T(8,128)(2,1)S(1)} %copy-done, bf16[48,128,128]{2,1,0:T(8,128)(2,1)} %param.9), kind=kOutput, calls=%fused_computation.6 | convolution fusion | flops 202113024 | bytes 4718592 | tf_op jit(solution)/shard_map/cij,cjr->cir/dot_general | solution.py:53
  4.0 0.0 copy-done.1
  4.0 2.9 %convolution_bitcast_fusion = f32[48,128,128]{1,2,0:T(8,128)} fusion(bf16[48,128,128]{2,1,0:T(8,128)(2,1)S(1)} %convolution_convert_fusion.1, bf16[48,128,128]{2,1,0:T(8,128)(2,1)S(1)} %copy-done.1), kind=kOutput, calls=%fused_computation.4 | convolution fusion | flops 201326592 | bytes 6291456 | tf_op jit(solution)/shard_map/cij,cjr->cir/dot_general | solution.py:53
  7.0 0.0 copy-start.4
  7.0 3.6 %copy.32 = f32[48,128,128]{2,0,1:T(8,128)} copy(f32[48,128,128]{1,2,0:T(8,128)} %convolution_bitcast_fusion) | data formatting | bytes 6291456 | tf_op jit(solution)/shard_map/cij,cjr->cir/dot_general | solution.py:53
  10.6 0.0 copy-done.4
  10.6 3.9 %fusion.16 = f32[64,128,128]{2,0,1:T(8,128)S(1)} fusion(f32[48,128,128]{2,0,1:T(8,128)} %copy.32, s32[48]{0:T(128)S(1)} %copy-done.4), kind=kOutput, calls=%fused_computation.20 | convolution fusion | flops 603982848 | bytes 7340224 | tf_op jit(solution)/shard_map/cp,cwr->pwr/dot_general | solution.py:74
  14.5 0.6 copy.49
  15.0 11.0 %all_to_all.25 = f32[2,32,1,128,128]{4,1,3,2,0:T(8,128)} all-to-all(f32[2,32,1,128,128]{4,1,3,2,0:T(8,128)S(1)} %bitcast.52), channel_id=1, replica_groups=mesh['row'=4,'col_0'=4,'col_1'=8,'col_2'=2] {'col_2'}, dimensions={0} | all-to-all | bytes 8388608 | tf_op jit(solution)/shard_map/all_to_all | solution.py:19
  26.0 4.2 %reduce_sum.31 = f32[32,128,128]{2,0,1:T(8,128)} reduce(f32[2,32,1,128,128]{4,1,3,2,0:T(8,128)} %all_to_all.25, f32[]{:T(128)} %constant.16.clone.1), dimensions={0,2}, to_apply=%region_0.0 | reduce | flops 524288 | bytes 6291460 | tf_op jit(solution)/shard_map/reduce_sum | solution.py:20
  30.2 2.8 %copy.35 = f32[32,1,128,128]{3,2,1,0:T(8,128)S(1)} copy(f32[32,1,128,128]{3,0,2,1:T(8,128)} %bitcast.53) | data formatting | bytes 4194304 | tf_op jit(solution)/shard_map/reduce_sum | solution.py:20
  33.0 57.1 %all_to_all.26 = f32[32,1,128,128]{3,2,1,0:T(8,128)} all-to-all(f32[32,1,128,128]{3,2,1,0:T(8,128)S(1)} %copy.35), channel_id=1, replica_groups=mesh['row'=4,'col_0'=4,'col_1'=8,'col_2'=2] {'col_0','col_1'}, dimensions={0} | all-to-all | bytes 4194304 | tf_op jit(solution)/shard_map/all_to_all | solution.py:26
  90.1 0.0 copy-start.2
  90.1 0.0 copy-start.3
  90.1 1.7 %reduce_sum.33 = f32[128,128]{1,0:T(8,128)S(1)} reduce(f32[32,1,128,128]{3,2,1,0:T(8,128)} %all_to_all.26, f32[]{:T(128)} %constant.16.clone.1), dimensions={0,1}, to_apply=%region_1.0 | reduce | flops 507904 | bytes 2162692 | tf_op jit(solution)/shard_map/reduce_sum | solution.py:26
  91.9 9.3 %all_to_all.27 = f32[4,1,128,128]{3,2,1,0:T(8,128)S(1)} all-to-all(f32[4,1,128,128]{3,2,1,0:T(8,128)S(1)} %broadcast_in_dim.35), channel_id=1, replica_groups=mesh['row'=4,'col_0'=4,'col_1'=8,'col_2'=2] {'row'}, dimensions={0} | all-to-all | bytes 524288 | tf_op jit(solution)/shard_map/all_to_all | solution.py:31
  101.2 0.0 copy-done.2
  101.3 0.0 copy-done.3
  101.3 1.1 convolution_convert_fusion.2
  102.3 0.1 copy.36
  102.4 1.2 broadcast_in_dim.36
  103.7 8.2 %all-to-all-start.3 = ((bf16[32,1,128,128]{3,2,1,0:T(8,128)(2,1)}), bf16[32,1,128,128]{3,2,1,0:T(8,128)(2,1)}, u32[]{:S(2)}, u32[]{:S(2)}) async-start(bf16[32,1,128,128]{3,2,1,0:T(8,128)(2,1)} %broadcast_in_dim.36), calls=%async_computation.3 | async-start | bytes 2097152 | tf_op jit(solution)/shard_map/all_to_all | solution.py:31
  111.9 0.7 copy.42
  112.6 22.8 %all-to-all-done.3 = bf16[32,1,128,128]{3,2,1,0:T(8,128)(2,1)} async-done(((bf16[32,1,128,128]{3,2,1,0:T(8,128)(2,1)}), bf16[32,1,128,128]{3,2,1,0:T(8,128)(2,1)}, u32[]{:S(2)}, u32[]{:S(2)}) %all-to-all-start.3) | async-done | bytes 1048608 | tf_op jit(solution)/shard_map/all_to_all | solution.py:31
  135.5 1.7 %broadcast_in_dim.38 = bf16[2,32,1,128,128]{4,3,1,2,0:T(8,128)(2,1)S(1)} broadcast(bf16[32,128,128]{2,1,0:T(8,128)(2,1)} %bitcast.10), dimensions={1,3,4} | broadcast | bytes 3145728 | tf_op jit(solution)/shard_map/broadcast_in_dim | solution.py:31
  137.2 11.0 %all_to_all.28 = bf16[2,32,1,128,128]{4,3,1,2,0:T(8,128)(2,1)S(1)} all-to-all(bf16[2,32,1,128,128]{4,3,1,2,0:T(8,128)(2,1)S(1)} %broadcast_in_dim.38), channel_id=1, replica_groups=mesh['row'=4,'col_0'=4,'col_1'=8,'col_2'=2] {'col_2'}, dimensions={0} | all-to-all | bytes 4194304 | tf_op jit(solution)/shard_map/all_to_all | solution.py:31
  148.2 1.5 copy.37
  149.7 3.5 %gather_fusion = bf16[48,128,128]{2,1,0:T(8,128)(2,1)} fusion(bf16[64,128,128]{2,1,0:T(8,128)(2,1)} %bitcast.54, s32[1024]{0:T(1024)S(1)} %pad_clamp_fusion), kind=kCustom, calls=%fused_computation | custom fusion | bytes 3145920 | tf_op jit(solution)/shard_map/jit(_take)/gather | solution.py:81
  153.3 5.3 %fusion.3 = bf16[48,128,128]{1,2,0:T(8,128)(2,1)} fusion(bf16[48,128,128]{2,1,0:T(8,128)(2,1)} %param.13, bf16[48,128,128]{2,1,0:T(8,128)(2,1)S(1)} %convolution_convert_fusion.1, bf16[48,128,128]{2,1,0:T(8,128)(2,1)} %param.14, bf16[48,128,128]{2,1,0:T(8,128)(2,1)} %gather_fusion, pred[48]{0:T(512)(128)(4,1)S(1)} %compare_and_fusion), kind=kOutput, calls=%fused_computation.9 | convolution fusion | flops 406585344 | bytes 7864368 | tf_op jit(solution)/shard_map/cij,cjr->cir/dot_general | solution.py:53
  158.6 2.6 %copy.41 = bf16[48,128,128]{2,1,0:T(8,128)(2,1)} copy(bf16[48,128,128]{1,2,0:T(8,128)(2,1)} %fusion.3) | data formatting | bytes 3145728
  (5 shorter events, 0.1 us)
Async XLA Ops:
  0.6 1.4 copy-start
  0.6 3.4 %copy-start.1 = (bf16[48,128,128]{2,1,0:T(8,128)(2,1)S(1)}, bf16[48,128,128]{2,1,0:T(8,128)(2,1)}, u32[]{:S(2)}) copy-start(bf16[48,128,128]{2,1,0:T(8,128)(2,1)} %param.12) | copy-start | bytes 4718596
  7.0 3.6 %copy-start.4 = (s32[48]{0:T(128)S(1)}, s32[48]{0:T(128)}, u32[]{:S(2)}) copy-start(s32[48]{0:T(128)} %param.17) | copy-start | bytes 580
  90.1 11.1 %copy-start.2 = (bf16[1,128,128]{2,1,0:T(8,128)(2,1)S(1)}, bf16[1,128,128]{2,1,0:T(8,128)(2,1)}, u32[]{:S(2)}) copy-start(bf16[1,128,128]{2,1,0:T(8,128)(2,1)} %param.10) | copy-start | bytes 98308
  90.1 11.1 %copy-start.3 = (bf16[1,128,128]{2,1,0:T(8,128)(2,1)S(1)}, bf16[1,128,128]{2,1,0:T(8,128)(2,1)}, u32[]{:S(2)}) copy-start(bf16[1,128,128]{2,1,0:T(8,128)(2,1)} %param.16) | copy-start | bytes 98308
  103.7 31.8 %all-to-all-start.3 = ((bf16[32,1,128,128]{3,2,1,0:T(8,128)(2,1)}), bf16[32,1,128,128]{3,2,1,0:T(8,128)(2,1)}, u32[]{:S(2)}, u32[]{:S(2)}) async-start(bf16[32,1,128,128]{3,2,1,0:T(8,128)(2,1)} %broadcast_in_dim.36), calls=%async_computation.3 | async-start | bytes 2097152 | tf_op jit(solution)/shard_map/all_to_all | solution.py:31
where the time goes:
time: 162 us; the launch traced here: 161 us
  blocking collectives  88.5 us (55%)
  waiting for transfers between devices  22.8 us (14%)
  local copies, waits for them, and re-layouts  19.8 us (12%)
  matrix products  15.2 us (9%)
  starting transfers between devices  8.2 us (5%)
  other arithmetic  5.93 us (4%)
    all_to_all x1, blocking collectives, summed_rows(): return jnp.sum(lax.all_to_all(own, far, 0, 0, tiled=True), axis=0)  57.1 us
    all_to_all x1, waiting for transfers between devices, from_everyone(): lax.all_to_all(jnp.broadcast_to(x[None], (count, *x.shape)), axis, 0, 0,...  22.8 us
    all_to_all x2, blocking collectives, from_everyone(): lax.all_to_all(jnp.broadcast_to(x[None], (count, *x.shape)), axis, 0, 0,...  20.4 us
    dot_general x4, matrix products, product(): jnp.einsum('cij,cjr->cir', mats, vals, preferred_element_type=jnp.float32)  11.3 us
    all_to_all x1, blocking collectives, summed_on_arrival(): lax.all_to_all(pieces, axis, split_axis=0, concat_axis=0, tiled=True)  11 us
    all_to_all x1, starting transfers between devices, from_everyone(): lax.all_to_all(jnp.broadcast_to(x[None], (count, *x.shape)), axis, 0, 0,...  8.2 us
    unnamed x12, local copies, waits for them, and re-layouts  4.71 us
    reduce_sum x1, other arithmetic, summed_on_arrival(): return arrived.sum(axis=0)  4.18 us
  transfers between devices with their start and end apart: 1, of which 1 were waited for; matrix products, arithmetic and copies ran while one was open for 0% of the time, Pallas kernels for 0%

commit v1 on v0

v1 whole, which is shorter than its diff:
```python
import functools

import jax
import jax.numpy as jnp
from jax import lax
from jax.experimental import pallas as pl
from jax.experimental.pallas import tpu as pltpu
from jax.sharding import PartitionSpec as P

BF = jnp.bfloat16
F32 = jnp.float32
MESH = pl.DeviceIdType.MESH
NCH = 48
GRP = 8
CHUNKS = NCH // GRP
NT = (((1,), (1,)), ((), ()))
TN = (((0,), (1,)), ((), ()))


def mm(a, b):
    return jnp.dot(a, b, preferred_element_type=F32)


def mm_nt(a, b):
    return lax.dot_general(a, b, NT, preferred_element_type=F32)


def loop(n, body, unroll=1):
    def step(i, carry):
        body(i)
        return carry

    lax.fori_loop(0, n, step, 0, unroll=unroll)


def kernel(
    tbl,
    po,
    rhs_h,
    prhs_h,
    linv_h,
    loff_h,
    uinv_h,
    uoff_h,
    plinv_h,
    puinv_h,
    out_h,
    psol_h,
    rhs,
    linv,
    loff,
    uinv,
    uoff,
    prhs,
    plinv,
    puinv,
    fwd,
    run,
    own,
    sib,
    sibr,
    snd,
    r1p,
    r1m,
    fp,
    fm,
    snd2,
    r2p,
    r2m,
    gp,
    gm,
    snd3,
    zr,
    prt,
    gath,
    ufwd,
    mat,
    outv,
    psolv,
    load_sem,
    out_sem,
    send_sem,
    recv_sem,
):
    x = lax.axis_index("row")
    col = lax.axis_index("col")
    core = lax.rem(col, 2)
    z = lax.rem(lax.div(col, 2), 8)
    y = lax.div(col, 16)
    flip = 1 - core
    a = flip * x + core * y
    b = flip * y + core * x

    def at_ab(a_, b_):
        x_ = flip * a_ + core * b_
        y_ = flip * b_ + core * a_
        return (x_, y_ * 16 + z * 2 + core)

    ap, am, ao = lax.rem(a + 1, 4), lax.rem(a + 3, 4), lax.rem(a + 2, 4)
    bp, bm, bo = lax.rem(b + 1, 4), lax.rem(b + 3, 4), lax.rem(b + 2, 4)
    d_ap, d_am, d_bp, d_bm = at_ab(ap, b), at_ab(am, b), at_ab(a, bp), at_ab(a, bm)
    d_sib = (x, y * 16 + z * 2 + flip)
    zs = [lax.rem(z + d, 8) for d in range(8)]
    d_z = [(x, y * 16 + zs[d] * 2 + core) for d in range(8)]

    barrier = pltpu.get_barrier_semaphore()
    peers = [d_sib, d_ap, d_am, d_bp, d_bm] + d_z[1:]
    for peer in peers:
        pl.semaphore_signal(barrier, inc=1, device_id=peer, device_id_type=MESH)

    loads = []

    def load(src, dst):
        cp = pltpu.make_async_copy(src, dst, load_sem.at[len(loads)])
        cp.start()
        loads.append(cp)
        return cp

    chunk_loads = []
    for k in range(CHUNKS):
        part = pl.ds(k * GRP, GRP)
        chunk_loads.append(
            [
                load(linv_h.at[part], linv.at[part]),
                load(rhs_h.at[part], rhs.at[part]),
                load(loff_h.at[part], loff.at[part]),
            ]
        )
    parent_loads = [load(prhs_h, prhs), load(plinv_h, plinv), load(puinv_h, puinv)]
    upper_loads = [load(uinv_h, uinv), load(uoff_h, uoff)]

    run[NCH] = jnp.zeros((128, 128), F32)

    for k in range(CHUNKS):
        for cp in chunk_loads[k]:
            cp.wait()

        def forward(i, k=k):
            c0 = k * GRP + i * 4
            terms = []
            for j in range(4):
                f = mm(linv[c0 + j], rhs[c0 + j]).astype(BF)
                fwd[c0 + j] = f
                terms.append(mm_nt(f.T, loff[c0 + j]))
            for j in range(4):
                run[c0 + j] = terms[j] + run[tbl[c0 + j]]

        loop(GRP // 4, forward)

    def place(h, j):
        yy, zz = lax.div(j, 8), lax.rem(j, 8)
        base = (1 - h) * j + h * (yy * 32 + zz)
        stride = (1 - h) * 32 + h * 8
        return base, stride

    def pack(h, ref, dtype):
        def body(j):
            v = run[tbl[NCH + 2 * j + h]]
            base, stride = place(h, j)
            for q in range(4):
                ref[base + q * stride] = v[32 * q : 32 * q + 32].astype(dtype)

        loop(32, body, unroll=2)

    pack(flip, sib, BF)
    pl.semaphore_wait(barrier, len(peers))

    sends = []

    def remote(src, dst, slot, dev):
        return pltpu.make_async_remote_copy(
            src_ref=src,
            dst_ref=dst,
            send_sem=send_sem.at[slot],
            recv_sem=recv_sem.at[slot],
            device_id=dev,
            device_id_type=MESH,
        )

    def send(src, dst, slot, dev):
        cp = remote(src, dst, slot, dev)
        cp.start()
        sends.append(cp)

    def arrived(dst, slot):
        remote(dst, dst, slot, d_sib).wait_recv()

    def half(i, h):
        return pl.ds(i * 32 + h * 16, 16)

    order = lambda m: [
        (lax.rem(m + 2, 4), 0),
        (lax.rem(m + 2, 4), 1),
        (lax.rem(m + 1, 4), 1),
        (lax.rem(m + 3, 4), 0),
        (lax.rem(m + 1, 4), 0),
        (lax.rem(m + 3, 4), 1),
        (m, 0),
        (m, 1),
    ]
    for s, (i, h) in enumerate(order(b)):
        send(sib.at[half(i, h)], sibr.at[half(i, h)], s, d_sib)
    pack(core, own, F32)

    def from_sib(s):
        i, h = order(a)[s]
        arrived(sibr.at[half(i, h)], s)

    def joined(i, h, more=None):
        def body(n):
            u = i * 32 + h * 16 + n
            v = own[u] + sibr[u].astype(F32)
            if more is not None:
                v = v + more[n].astype(F32)
            snd[u] = v.astype(BF)

        loop(16, body, unroll=4)

    A, B = pl.ds(0, 16), pl.ds(16, 16)
    from_sib(0)
    joined(ao, 0)
    send(snd.at[half(ao, 0)], r1p, 8, d_ap)
    from_sib(1)
    joined(ao, 1)
    send(snd.at[half(ao, 1)], r1m, 9, d_am)
    from_sib(2)
    joined(ap, 1)
    send(snd.at[half(ap, 1)], fp.at[B], 10, d_ap)
    from_sib(3)
    joined(am, 0)
    send(snd.at[half(am, 0)], fm.at[A], 11, d_am)
    from_sib(4)
    arrived(r1p, 8)
    joined(ap, 0, r1p)
    send(snd.at[half(ap, 0)], fp.at[A], 12, d_ap)
    from_sib(5)
    arrived(r1m, 9)
    joined(am, 1, r1m)
    send(snd.at[half(am, 1)], fm.at[B], 13, d_am)
    from_sib(6)
    from_sib(7)
    arrived(fp.at[B], 10)
    arrived(fm.at[A], 11)
    arrived(fp.at[A], 12)
    arrived(fm.at[B], 13)

    def at_a(n):
        u = a * 32 + n
        return own[u] + sibr[u].astype(F32) + fp[n].astype(F32) + fm[n].astype(F32)

    def half2(i, h):
        return pl.ds(i * 8 + h * 4, 4)

    def joined2(i, h, more=None):
        for n in range(4):
            u = i * 8 + h * 4 + n
            v = at_a(u)
            if more is not None:
                v = v + more[n].astype(F32)
            snd2[u] = v.astype(BF)

    A2, B2 = pl.ds(0, 4), pl.ds(4, 4)
    joined2(bo, 0)
    send(snd2.at[half2(bo, 0)], r2p, 14, d_bp)
    joined2(bo, 1)
    send(snd2.at[half2(bo, 1)], r2m, 15, d_bm)
    joined2(bp, 1)
    send(snd2.at[half2(bp, 1)], gp.at[B2], 16, d_bp)
    joined2(bm, 0)
    send(snd2.at[half2(bm, 0)], gm.at[A2], 17, d_bm)
    arrived(r2p, 14)
    joined2(bp, 0, r2p)
    send(snd2.at[half2(bp, 0)], gp.at[A2], 18, d_bp)
    arrived(r2m, 15)
    joined2(bm, 1, r2m)
    send(snd2.at[half2(bm, 1)], gm.at[B2], 19, d_bm)
    arrived(gp.at[B2], 16)
    arrived(gm.at[A2], 17)
    arrived(gp.at[A2], 18)
    arrived(gm.at[B2], 19)

    def at_b(i):
        return at_a(b * 8 + i) + gp[i].astype(F32) + gm[i].astype(F32)

    for d in (4, 3, 5, 2, 6, 1, 7):
        snd3[d - 1] = at_b(zs[d]).astype(BF)
        send(snd3.at[d - 1], zr.at[d - 1], 20 + d - 1, d_z[d])

    for cp in parent_loads:
        cp.wait()
    prt[...] = prhs[0].astype(F32).T
    for cp in upper_loads:
        cp.wait()

    def prepare(i):
        for j in range(4):
            c = i * 4 + j
            ui = uinv[c]
            ufwd[c] = mm(ui, fwd[c])
            mat[c] = mm(ui, uoff[c]).astype(BF)

    loop(NCH // 4, prepare)

    total = at_b(z)
    for d in range(1, 8):
        arrived(zr.at[d - 1], 20 + d - 1)
        total = total + zr[d - 1].astype(F32)

    res = (prt[pl.ds(x * 32, 32), :] - total).astype(BF)
    pf = mm_nt(res, plinv[0]).astype(BF)
    base = core * 128
    me = base + a * 32 + b * 8 + z
    gath[me] = mm_nt(pf, puinv[0]).astype(BF)

    for d in (4, 3, 5, 2, 6, 1, 7):
        send(gath.at[me], gath.at[me], 27 + d - 1, d_z[d])
    for d in range(1, 8):
        arrived(gath.at[base + a * 32 + b * 8 + zs[8 - d]], 27 + d - 1)

    def both(ref_slice, slot, dev):
        send(gath.at[ref_slice], gath.at[ref_slice], slot, dev)

    def bsl(i, start=0, n=8):
        return pl.ds(base + a * 32 + i * 8 + start, n)

    both(bsl(b), 34, d_bp)
    both(bsl(b), 35, d_bm)
    arrived(gath.at[bsl(bm)], 34)
    both(bsl(bm, 0, 4), 36, d_bp)
    arrived(gath.at[bsl(bp)], 35)
    both(bsl(bp, 4, 4), 37, d_bm)
    arrived(gath.at[bsl(bo, 0, 4)], 36)
    arrived(gath.at[bsl(bo, 4, 4)], 37)

    def asl(i, start=0, n=32, bs=base):
        return pl.ds(bs + i * 32 + start, n)

    both(asl(a), 38, d_ap)
    both(asl(a), 39, d_am)
    both(asl(a), 42, d_sib)
    arrived(gath.at[asl(am)], 38)
    both(asl(am, 0, 16), 40, d_ap)
    both(asl(am), 43, d_sib)
    arrived(gath.at[asl(ap)], 39)
    both(asl(ap, 16, 16), 41, d_am)
    both(asl(ap), 44, d_sib)
    arrived(gath.at[asl(ao, 0, 16)], 40)
    both(asl(ao, 0, 16), 45, d_sib)
    arrived(gath.at[asl(ao, 16, 16)], 41)
    both(asl(ao, 16, 16), 46, d_sib)
    other = flip * 128
    arrived(gath.at[asl(b, bs=other)], 42)
    arrived(gath.at[asl(bm, bs=other)], 43)
    arrived(gath.at[asl(bp, bs=other)], 44)
    arrived(gath.at[asl(bo, 0, 16, other)], 45)
    arrived(gath.at[asl(bo, 16, 16, other)], 46)

    def parent(p):
        h = lax.rem(p, 2)
        first, stride = place(h, lax.div(p, 2))
        return jnp.concatenate(
            [gath[h * 128 + first + q * stride] for q in range(4)], axis=0
        )

    psolv[0] = parent(col).T
    pcopy = pltpu.make_async_copy(psolv, psol_h, out_sem.at[CHUNKS])
    pcopy.start()

    copies = [pcopy]
    for k in range(CHUNKS):

        def backward(i, k=k):
            for j in range(4):
                c = k * GRP + i * 4 + j
                outv[c] = (ufwd[c] - mm_nt(mat[c], parent(po[c]))).astype(BF)

        loop(GRP // 4, backward)
        part = pl.ds(k * GRP, GRP)
        cp = pltpu.make_async_copy(outv.at[part], out_h.at[part], out_sem.at[k])
        cp.start()
        copies.append(cp)
    for cp in sends:
        cp.wait_send()
    for cp in copies:
        cp.wait()


def on_device(
    child_rhs,
    parent_rhs,
    child_lower_inv,
    child_lower_off,
    child_upper_inv,
    child_upper_off,
    parent_lower_inv,
    parent_upper_inv,
    parent_of,
):
    n = child_rhs.shape[0]
    n_par = 64
    ids = jnp.arange(n, dtype=jnp.int32)
    label = jnp.concatenate([parent_of, jnp.arange(n_par, dtype=jnp.int32)])
    limit = jnp.concatenate([ids, jnp.full((n_par,), n, jnp.int32)])
    hit = (label[:, None] == parent_of[None, :]) & (ids[None, :] < limit[:, None])
    last = jnp.max(jnp.where(hit, ids[None, :], -1), axis=1)
    tbl = jnp.where(last < 0, n, last)

    mats = lambda: pltpu.VMEM((NCH, 128, 128), BF)
    one = lambda: pltpu.VMEM((1, 128, 128), BF)
    units = lambda k, dtype=BF: pltpu.VMEM((k, 32, 128), dtype)
    smem = pl.BlockSpec(memory_space=pltpu.SMEM)
    hbm = pl.BlockSpec(memory_space=pl.ANY)
    return pl.pallas_call(
        kernel,
        out_shape=(
            jax.ShapeDtypeStruct(child_rhs.shape, BF),
            jax.ShapeDtypeStruct(parent_rhs.shape, BF),
        ),
        in_specs=[smem, smem] + [hbm] * 8,
        out_specs=(hbm, hbm),
        scratch_shapes=[
            mats(),
            mats(),
            mats(),
            mats(),
            mats(),
            one(),
            one(),
            one(),
            mats(),
            pltpu.VMEM((NCH + 1, 128, 128), F32),
            units(128, F32),
            units(128),
            units(128),
            units(128),
            units(16),
            units(16),
            units(32),
            units(32),
            units(32),
            units(4),
            units(4),
            units(8),
            units(8),
            units(7),
            units(7),
            pltpu.VMEM((128, 128), F32),
            units(256),
            pltpu.VMEM((NCH, 128, 128), F32),
            mats(),
            mats(),
            one(),
            pltpu.SemaphoreType.DMA((3 * CHUNKS + 5,)),
            pltpu.SemaphoreType.DMA((CHUNKS + 1,)),
            pltpu.SemaphoreType.DMA((47,)),
            pltpu.SemaphoreType.DMA((47,)),
        ],
        compiler_params=pltpu.CompilerParams(
            collective_id=0, has_side_effects=True, vmem_limit_bytes=60 * 2**20
        ),
    )(
        tbl,
        parent_of,
        child_rhs,
        parent_rhs,
        child_lower_inv,
        child_lower_off,
        child_upper_inv,
        child_upper_off,
        parent_lower_inv,
        parent_upper_inv,
    )


def solution(mesh):
    child = P(("row", "col"), None, None)
    par = P("col", None, None)
    return jax.shard_map(
        on_device,
        mesh=mesh,
        in_specs=(child, par, child, child, child, child, par, par, P(("row", "col"))),
        out_specs=(child, par),
        check_vma=False,
    )
```

time: 162 us -> 67.5 us (0.42)
  blocking collectives: 88.5 us -> 0 us
  Pallas kernels: 0 us -> 60.6 us
  waiting for transfers between devices: 22.8 us -> 0 us
  local copies, waits for them, and re-layouts: 19.8 us -> 3.35 us
  matrix products: 15.2 us -> 0 us
  starting transfers between devices: 8.2 us -> 0 us
  other arithmetic: 5.93 us -> 2.01 us
    all_to_all x4 -> x0, blocking collectives: 88.5 us -> none  [the longest x1 57.1 us: summed_rows(): return jnp.sum(lax.all_to_all(own, far, 0, 0, tiled=True), axis=0)]
    pallas_call x0 -> x1, Pallas kernels: none -> 60.6 us  [on_device(): pl.pallas_call(kernel, out_shape=(jax.ShapeDtypeStruct(child_rhs.shape, B...]
    all_to_all x1 -> x0, waiting for transfers between devices: 22.8 us -> none  [from_everyone(): lax.all_to_all(jnp.broadcast_to(x[None], (count, *x.shape)), axis, 0, 0,...]
    dot_general x5 -> x0, matrix products: 15.2 us -> none  [the longest x4 11.3 us: product(): jnp.einsum('cij,cjr->cir', mats, vals, preferred_element_type=jnp.float32)]
    all_to_all x1 -> x0, starting transfers between devices: 8.2 us -> none  [from_everyone(): lax.all_to_all(jnp.broadcast_to(x[None], (count, *x.shape)), axis, 0, 0,...]
    reduce_sum x3 -> x0, other arithmetic: 5.91 us -> none  [the longest x1 4.18 us: summed_on_arrival(): return arrived.sum(axis=0)]
    dot_general x1 -> x0, local copies, waits for them, and re-layouts: 3.6 us -> none  [product(): jnp.einsum('cij,cjr->cir', mats, vals, preferred_element_type=jnp.float32)]
    gather x1 -> x0, local copies, waits for them, and re-layouts: 3.53 us -> none  [on_device(): picked = jnp.take(gathered, parent_of, axis=0)]
  transfers between devices with their start and end apart: 1 -> 0, of which waited for: 1 -> 0; matrix products, arithmetic and copies ran while one was open for 0% -> 0% of each run, Pallas kernels for 0% -> 0%
where the time goes in v1:
time: 67.5 us; the launch traced here: 66.6 us
  Pallas kernels  60.6 us (90%)
  local copies, waits for them, and re-layouts  3.35 us (5%)
  other arithmetic  2.01 us (3%)
    pallas_call x1, Pallas kernels, on_device(): pl.pallas_call(kernel, out_shape=(jax.ShapeDtypeStruct(child_rhs.shape, B...  60.6 us
    unnamed x4, local copies, waits for them, and re-layouts  3.35 us

profile of v1, /device:TPU:1, one launch (start us, length us, event | category | flops | bytes accessed | tf_op | source)
XLA Modules:
  0.0 66.6 jit_solution(10500102479789344376)
XLA Ops:
  0.6 0.7 %pad_add_fusion = s32[112]{0:T(128)S(1)} fusion(s32[64]{0:T(128)S(1)} %iota.7, s32[48]{0:T(128)} %po.1), kind=kLoop, calls=%fused_computation.4 | loop fusion | flops 112 | bytes 896 | tf_op jit(solution)/shard_map/concatenate | solution.py:402
  1.4 0.8 %select_reduce_fusion = s32[112]{0:T(128)S(1)} fusion(s32[112]{0:T(128)} %constant.1.clone.1, s32[112]{0:T(128)S(1)} %pad_add_fusion, s32[48]{0:T(128)} %po.1), kind=kLoop, calls=%fused_computation | loop fusion | flops 26768 | bytes 1536 | tf_op jit(solution)/shard_map/reduce_max | solution.py:405
  2.1 0.5 compare_select_fusion.tbl
  2.6 60.6 %shard_map.104 = (bf16[48,128,128]{2,1,0:T(8,128)(2,1)}, bf16[1,128,128]{2,1,0:T(8,128)(2,1)}) custom-call(s32[112]{0:T(128)} %compare_select_fusion.tbl, s32[48]{0:T(128)} %po.1, bf16[48,128,128]{2,1,0:T(8,128)(2,1)} %rhs_h.1, bf16[1,128,128]{2,1,0:T(8,128)(2,1)} %prhs_h.1, bf16[48,128,128]{2,1,0:T(8,128)(2,1)} %linv_h.1, bf16[48,128,128]{2,1,0:T(8,128)(2,1)} %loff_h.1, ...), custom_call_target="tpu_custom_call" | custom-call | tf_op jit(solution)/shard_map/pallas_call | solution.py:413
  63.3 0.0 copy-start
  63.3 2.7 %copy.13 = bf16[48,128,128]{2,1,0:T(8,128)(2,1)} copy(bf16[48,128,128]{2,1,0:T(8,128)(2,1)} %get-tuple-element.4) | data formatting | bytes 3145728
  66.0 0.0 copy-done
  66.0 0.6 copy.14
  (1 shorter events, 0.0 us)
Async XLA Ops:
  63.3 2.7 %copy-start = (bf16[1,128,128]{2,1,0:T(8,128)(2,1)S(1)}, bf16[1,128,128]{2,1,0:T(8,128)(2,1)}, u32[]{:S(2)}) copy-start(bf16[1,128,128]{2,1,0:T(8,128)(2,1)} %get-tuple-element.5) | copy-start | bytes 98308

commit v2 on v0

v2 whole, which is shorter than its diff:
```python
import jax
import jax.numpy as jnp
from jax import lax
from jax.experimental import pallas as pl
from jax.experimental.pallas import tpu as pltpu
from jax.sharding import PartitionSpec as P

BF = jnp.bfloat16
F32 = jnp.float32
MESH = pl.DeviceIdType.MESH
NCH = 48
GRP = 8
CHUNKS = NCH // GRP
NT = (((1,), (1,)), ((), ()))


def mm(a, b):
    return jnp.dot(a, b, preferred_element_type=F32)


def mm_nt(a, b):
    return lax.dot_general(a, b, NT, preferred_element_type=F32)


def loop(n, body, unroll=1):
    def step(i, carry):
        body(i)
        return carry

    lax.fori_loop(0, n, step, 0, unroll=unroll)


def forward_kernel(
    po_h,
    rhs_h,
    prhs_h,
    linv_h,
    loff_h,
    uinv_h,
    uoff_h,
    plinv_h,
    puinv_h,
    gath,
    ufwd,
    mat,
    rhs,
    linv,
    loff,
    uinv,
    uoff,
    prhs,
    plinv,
    puinv,
    fwd,
    run,
    pov,
    tabv,
    tab,
    sib,
    sibr,
    snd,
    r1,
    fin,
    snd2,
    gin,
    snd3,
    zr_out,
    zr,
    prt,
    load_sem,
    tab_sem,
    send_sem,
    recv_sem,
):
    x = lax.axis_index("row")
    col = lax.axis_index("col")
    core = lax.rem(col, 2)
    z = lax.rem(lax.div(col, 2), 8)
    y = lax.div(col, 16)
    flip = 1 - core

    def dev(x_, y_, z_, c_):
        return (x_, y_ * 16 + z_ * 2 + c_)

    def mod4(v):
        return lax.rem(v, 4)

    d_sib = dev(x, y, z, flip)
    d_x = [dev(mod4(x + d), y, z, core) for d in range(4)]
    d_y = [dev(x, mod4(y + d), z, core) for d in range(4)]
    zs = [lax.rem(z + d, 8) for d in range(8)]
    d_z = [dev(x, y, zs[d], core) for d in range(8)]
    d_a, d_b = (d_x, d_y), (d_y, d_x)
    ax = [[mod4(x + d) for d in range(4)], [mod4(y + d) for d in range(4)]]
    bx = [ax[1], ax[0]]

    barrier = pltpu.get_barrier_semaphore()
    peers = [d_sib] + d_x[1:] + d_y[1:] + d_z[1:]
    for peer in peers:
        pl.semaphore_signal(barrier, inc=1, device_id=peer, device_id_type=MESH)

    loads, sends, pend = [], [], {}

    def load(src, dst):
        cp = pltpu.make_async_copy(src, dst, load_sem.at[len(loads)])
        cp.start()
        loads.append(cp)
        return cp

    po_load = load(po_h, pov)
    chunk_loads = []
    for k in range(CHUNKS):
        part = pl.ds(k * GRP, GRP)
        chunk_loads.append(
            [
                load(linv_h.at[part], linv.at[part]),
                load(rhs_h.at[part], rhs.at[part]),
                load(loff_h.at[part], loff.at[part]),
            ]
        )
    parent_loads = [load(prhs_h, prhs), load(plinv_h, plinv), load(puinv_h, puinv)]
    upper_loads = [load(uinv_h, uinv), load(uoff_h, uoff)]

    run[NCH] = jnp.zeros((128, 128), F32)

    po_load.wait()
    mine = jnp.concatenate(
        [pov[...], jnp.full((1, 128 - NCH), -1, jnp.int32)], axis=1
    )
    rows = jnp.broadcast_to(mine, (128, 128))
    lane = lax.broadcasted_iota(jnp.int32, (128, 128), 1)
    child = lax.broadcasted_iota(jnp.int32, (128, 128), 0)
    label = jnp.where(lane < 64, rows, lane - 64)
    hit = (rows.T == label) & (child < jnp.where(lane < 64, lane, NCH))
    last = jnp.max(jnp.where(hit, child, -1), axis=0, keepdims=True)
    tabv[...] = jnp.where(last < 0, NCH, last)
    tab_copy = pltpu.make_async_copy(tabv, tab, tab_sem.at[0])
    tab_copy.start()

    for k in range(CHUNKS):
        for cp in chunk_loads[k]:
            cp.wait()
        terms = []
        for c in range(k * GRP, (k + 1) * GRP):
            f = mm(linv[c], rhs[c]).astype(BF)
            fwd[c] = f
            terms.append(mm_nt(f.T, loff[c]))
        if k == 0:
            tab_copy.wait()
        for j in range(GRP):
            c = k * GRP + j
            run[c] = terms[j] + run[tab[0, c]]

    def mine_of(t, i, h, n, core_):
        b_, zz = h * 2 + lax.div(n, 4), t * 4 + lax.rem(n, 4)
        x_, y_ = (i, b_) if t == 0 else (b_, i)
        row = pl.multiple_of(x_ * 32, 32)
        last_ = tab[0, 64 + y_ * 16 + zz * 2 + core_]
        return run[last_, pl.ds(row, 32), :]

    def remote(src, dst, slot, dev_):
        return pltpu.make_async_remote_copy(
            src_ref=src,
            dst_ref=dst,
            send_sem=send_sem.at[slot],
            recv_sem=recv_sem.at[slot],
            device_id=dev_,
            device_id_type=MESH,
        )

    def send(src, dst, slot, dev_):
        cp = remote(src, dst, slot, dev_)
        cp.start()
        sends.append(cp)
        pend[slot] = src

    def arrived(dst, slot):
        remote(dst, dst, slot, d_sib).wait_recv()
        pend.pop(slot)

    slots = {}

    def slot(*key):
        return slots.setdefault(key, len(slots))

    def half(i, h):
        return pl.ds(i * 16 + h * 8, 8)

    both = (0, 1)
    order = [(2, 0), (2, 1), (1, 1), (3, 0), (1, 0), (3, 1), (0, 0), (0, 1)]

    for s, (d, h) in enumerate(order):
        for t in both:
            i = ax[t][d]

            def pack(n, t=t, i=i, h=h):
                u = i * 16 + h * 8 + n
                sib[t, u] = mine_of(t, i, h, n, flip).astype(BF)

            loop(8, pack, unroll=8)
            if s == 0 and t == 0:
                pl.semaphore_wait(barrier, len(peers))
            send(
                sib.at[t, half(i, h)], sibr.at[t, half(i, h)], slot("s0", t, s), d_sib
            )

    def from_sib(t, s):
        d, h = order[s]
        arrived(sibr.at[t, half(ax[t][d], h)], slot("s0", t, s))

    def joined(t, d, h, more=None):
        i = ax[t][d]

        def body(n):
            u = i * 16 + h * 8 + n
            v = mine_of(t, i, h, n, core) + sibr[t, u].astype(F32)
            if more is not None:
                v = v + more[n].astype(F32)
            snd[t, u] = v.astype(BF)

        loop(8, body, unroll=8)
        return snd.at[t, half(i, h)]

    H = [pl.ds(0, 8), pl.ds(8, 8)]
    for t in both:
        from_sib(t, 0)
        send(joined(t, 2, 0), r1.at[t, 0], slot("r1", t, 0), d_a[t][1])
        from_sib(t, 1)
        send(joined(t, 2, 1), r1.at[t, 1], slot("r1", t, 1), d_a[t][3])
    for t in both:
        from_sib(t, 2)
        send(joined(t, 1, 1), fin.at[t, 0, H[1]], slot("f", t, 0, 1), d_a[t][1])
        from_sib(t, 3)
        send(joined(t, 3, 0), fin.at[t, 1, H[0]], slot("f", t, 1, 0), d_a[t][3])
    for t in both:
        for s in (4, 5):
            from_sib(t, s)
    for t in both:
        arrived(r1.at[t, 0], slot("r1", t, 0))
        src = joined(t, 1, 0, r1.at[t, 0])
        send(src, fin.at[t, 0, H[0]], slot("f", t, 0, 0), d_a[t][1])
        arrived(r1.at[t, 1], slot("r1", t, 1))
        src = joined(t, 3, 1, r1.at[t, 1])
        send(src, fin.at[t, 1, H[1]], slot("f", t, 1, 1), d_a[t][3])
    for t in both:
        for s in (6, 7):
            from_sib(t, s)
    for t in both:
        arrived(fin.at[t, 0, H[1]], slot("f", t, 0, 1))
        arrived(fin.at[t, 1, H[0]], slot("f", t, 1, 0))

    def at_a(t, b_, zz):
        n = b_ * 4 + zz
        v = mine_of(t, ax[t][0], 0, n, core) + sibr[t, ax[t][0] * 16 + n].astype(F32)
        return v + fin[t, 0, n].astype(F32) + fin[t, 1, n].astype(F32)

    for t in both:
        arrived(fin.at[t, 0, H[0]], slot("f", t, 0, 0))
        arrived(fin.at[t, 1, H[1]], slot("f", t, 1, 1))
        for d in (2, 1, 3):
            for zz in range(4):
                snd2[t, d - 1, zz] = at_a(t, bx[t][d], zz).astype(BF)
            send(snd2.at[t, d - 1], gin.at[t, d - 1], slot("g", t, d), d_b[t][d])

    def at_b(t, zz):
        v = at_a(t, bx[t][0], zz)
        for d in range(3):
            v = v + gin[t, d, zz].astype(F32)
        return v

    near = lax.div(z, 4)
    tot = []
    for t in both:
        for d in (2, 1, 3):
            arrived(gin.at[t, d - 1], slot("g", t, d))
        for zz in range(4):
            snd3[t * 4 + zz] = at_b(t, zz)
    for d in (4, 3, 5, 2, 6, 1, 7):
        zr_out[d - 1] = snd3[zs[d]].astype(BF)
        send(zr_out.at[d - 1], zr.at[d - 1], slot("z", d), d_z[d])

    for cp in parent_loads:
        cp.wait()
    prt[...] = prhs[0].astype(F32).T
    for cp in upper_loads:
        cp.wait()

    def prepare(i):
        for j in range(4):
            c = i * 4 + j
            ui = uinv[c]
            ufwd[c] = mm(ui, fwd[c])
            mat[c] = mm(ui, uoff[c]).astype(BF)

    loop(NCH // 4, prepare)

    total = snd3[z]
    for d in range(1, 8):
        arrived(zr.at[d - 1], slot("z", d))
        total = total + zr[d - 1].astype(F32)

    res = (prt[pl.ds(pl.multiple_of(x * 32, 32), 32), :] - total).astype(BF)
    pf = mm_nt(res, plinv[0]).astype(BF)

    def unit(z_):
        t_ = lax.div(z_, 4)
        ab = (1 - t_) * (x * 4 + y) + t_ * (y * 4 + x)
        return (core * 2 + t_) * 64 + ab * 4 + lax.rem(z_, 4)

    me = unit(z)
    gath[me] = mm_nt(pf, puinv[0]).astype(BF)

    for d in (4, 3, 5, 2, 6, 1, 7):
        send(gath.at[me], gath.at[me], slot("bz", d), d_z[d])
    for d in (7, 1, 6, 2, 5, 3, 4):
        arrived(gath.at[unit(zs[8 - d])], slot("bz", d))

    def share(ref_slice, slot_, dev_):
        send(gath.at[ref_slice], gath.at[ref_slice], slot_, dev_)

    def bsl(t, d):
        return pl.ds((core * 2 + t) * 64 + ax[t][0] * 16 + bx[t][d] * 4, 4)

    for t in both:
        for d in (2, 1, 3):
            share(bsl(t, 0), slot("bb", t, d), d_b[t][d])
    for d in (1, 3, 2):
        for t in both:
            arrived(gath.at[bsl(t, 4 - d)], slot("bb", t, d))

    def asl(t, d, h, core_=core):
        return pl.ds((core_ * 2 + t) * 64 + ax[t][d] * 16 + h * 8, 8)

    def over(t, d, h):
        share(asl(t, d, h), slot("o", t, d, h), d_sib)

    for t in both:
        share(asl(t, 0, 0), slot("ba", t, 1, 0), d_a[t][1])
        share(asl(t, 0, 1), slot("ba", t, 3, 1), d_a[t][3])
    for t in both:
        share(asl(t, 0, 1), slot("ba", t, 1, 1), d_a[t][1])
        share(asl(t, 0, 0), slot("ba", t, 3, 0), d_a[t][3])
    for t in both:
        for h in (0, 1):
            over(t, 0, h)
    for t in both:
        arrived(gath.at[asl(t, 3, 0)], slot("ba", t, 1, 0))
        share(asl(t, 3, 0), slot("ba", t, 2, 0), d_a[t][1])
        arrived(gath.at[asl(t, 1, 1)], slot("ba", t, 3, 1))
        share(asl(t, 1, 1), slot("ba", t, 2, 1), d_a[t][3])
    for t in both:
        over(t, 3, 0)
        over(t, 1, 1)
    for t in both:
        arrived(gath.at[asl(t, 3, 1)], slot("ba", t, 1, 1))
        over(t, 3, 1)
        arrived(gath.at[asl(t, 1, 0)], slot("ba", t, 3, 0))
        over(t, 1, 0)
    for h in (0, 1):
        for t in both:
            arrived(gath.at[asl(t, 2, h)], slot("ba", t, 2, h))
            over(t, 2, h)
    for d in (0, 3, 1, 2):
        for h in (0, 1):
            for t in both:
                arrived(gath.at[asl(t, d, h, flip)], slot("o", t, d, h))
    for cp in sends:
        cp.wait_send()


def parent_of_units(gath, p):
    h, z, y = lax.rem(p, 2), lax.rem(lax.div(p, 2), 8), lax.div(p, 16)
    t = lax.div(z, 4)
    first = (h * 2 + t) * 64 + lax.rem(z, 4) + (1 - t) * y * 4 + t * y * 16
    stride = (1 - t) * 16 + t * 4
    return jnp.concatenate([gath[first + q * stride] for q in range(4)], axis=0)


def backward_kernel(po, gath, ufwd, mat, out_h, psol_h, out, psol, sem):
    psol[0] = parent_of_units(gath, lax.axis_index("col")).T
    copies = []

    def put(src, dst):
        cp = pltpu.make_async_copy(src, dst, sem.at[len(copies)])
        cp.start()
        copies.append(cp)

    put(psol, psol_h)
    for k in range(CHUNKS):
        for c in range(k * GRP, (k + 1) * GRP):
            s = parent_of_units(gath, po[c])
            out[c] = (ufwd[c] - mm_nt(mat[c], s)).astype(BF)
        part = pl.ds(k * GRP, GRP)
        put(out.at[part], out_h.at[part])
    for cp in copies:
        cp.wait()


def on_device(
    child_rhs,
    parent_rhs,
    child_lower_inv,
    child_lower_off,
    child_upper_inv,
    child_upper_off,
    parent_lower_inv,
    parent_upper_inv,
    parent_of,
):
    mats = lambda: pltpu.VMEM((NCH, 128, 128), BF)
    one = lambda: pltpu.VMEM((1, 128, 128), BF)
    units = lambda *k: pltpu.VMEM((*k, 32, 128), BF)
    smem = pl.BlockSpec(memory_space=pltpu.SMEM)
    vmem = pl.BlockSpec(memory_space=pltpu.VMEM)
    hbm = pl.BlockSpec(memory_space=pl.ANY)
    gath, ufwd, mat = pl.pallas_call(
        forward_kernel,
        out_shape=(
            jax.ShapeDtypeStruct((256, 32, 128), BF),
            jax.ShapeDtypeStruct((NCH, 128, 128), F32),
            jax.ShapeDtypeStruct((NCH, 128, 128), BF),
        ),
        in_specs=[hbm] * 9,
        out_specs=(vmem, vmem, vmem),
        scratch_shapes=[
            mats(),
            mats(),
            mats(),
            mats(),
            mats(),
            one(),
            one(),
            one(),
            mats(),
            pltpu.VMEM((NCH + 1, 128, 128), F32),
            pltpu.VMEM((1, NCH), jnp.int32),
            pltpu.VMEM((1, 128), jnp.int32),
            pltpu.SMEM((1, 128), jnp.int32),
            units(2, 64),
            units(2, 64),
            units(2, 64),
            units(2, 2, 8),
            units(2, 2, 16),
            units(2, 3, 4),
            units(2, 3, 4),
            pltpu.VMEM((8, 32, 128), F32),
            units(7),
            units(7),
            pltpu.VMEM((128, 128), F32),
            pltpu.SemaphoreType.DMA((3 * CHUNKS + 6,)),
            pltpu.SemaphoreType.DMA((1,)),
            pltpu.SemaphoreType.DMA((90,)),
            pltpu.SemaphoreType.DMA((90,)),
        ],
        compiler_params=pltpu.CompilerParams(
            collective_id=0, has_side_effects=True, vmem_limit_bytes=40 * 2**20
        ),
    )(
        *[
            pltpu.with_memory_space_constraint(v, pltpu.HBM)
            for v in (
                parent_of.reshape(1, NCH),
                child_rhs,
                parent_rhs,
                child_lower_inv,
                child_lower_off,
                child_upper_inv,
                child_upper_off,
                parent_lower_inv,
                parent_upper_inv,
            )
        ]
    )
    return pl.pallas_call(
        backward_kernel,
        out_shape=(
            jax.ShapeDtypeStruct(child_rhs.shape, BF),
            jax.ShapeDtypeStruct(parent_rhs.shape, BF),
        ),
        in_specs=[smem, vmem, vmem, vmem],
        out_specs=(hbm, hbm),
        scratch_shapes=[mats(), one(), pltpu.SemaphoreType.DMA((CHUNKS + 1,))],
        compiler_params=pltpu.CompilerParams(vmem_limit_bytes=16 * 2**20),
    )(parent_of, gath, ufwd, mat)


def solution(mesh):
    child = P(("row", "col"), None, None)
    par = P("col", None, None)
    return jax.shard_map(
        on_device,
        mesh=mesh,
        in_specs=(child, par, child, child, child, child, par, par, P(("row", "col"))),
        out_specs=(child, par),
        check_vma=False,
    )
```

time: 162 us -> 52.6 us (0.32)
  blocking collectives: 88.5 us -> 0 us
  Pallas kernels: 0 us -> 51.9 us
  waiting for transfers between devices: 22.8 us -> 0 us
  local copies, waits for them, and re-layouts: 19.8 us -> 0.01 us
  matrix products: 15.2 us -> 0 us
  starting transfers between devices: 8.2 us -> 0 us
  other arithmetic: 5.93 us -> 0 us
    all_to_all x4 -> x0, blocking collectives: 88.5 us -> none  [the longest x1 57.1 us: summed_rows(): return jnp.sum(lax.all_to_all(own, far, 0, 0, tiled=True), axis=0)]
    pallas_call x0 -> x2, Pallas kernels: none -> 51.9 us  [the longest x1 49.5 us: on_device(): pl.pallas_call(forward_kernel, out_shape=(jax.ShapeDtypeStruct((256, 32,...]
    all_to_all x1 -> x0, waiting for transfers between devices: 22.8 us -> none  [from_everyone(): lax.all_to_all(jnp.broadcast_to(x[None], (count, *x.shape)), axis, 0, 0,...]
    dot_general x5 -> x0, matrix products: 15.2 us -> none  [the longest x4 11.3 us: product(): jnp.einsum('cij,cjr->cir', mats, vals, preferred_element_type=jnp.float32)]
    all_to_all x1 -> x0, starting transfers between devices: 8.2 us -> none  [from_everyone(): lax.all_to_all(jnp.broadcast_to(x[None], (count, *x.shape)), axis, 0, 0,...]
    reduce_sum x3 -> x0, other arithmetic: 5.91 us -> none  [the longest x1 4.18 us: summed_on_arrival(): return arrived.sum(axis=0)]
    unnamed x12 -> x2, local copies, waits for them, and re-layouts: 4.71 us -> 0.01 us
    dot_general x1 -> x0, local copies, waits for them, and re-layouts: 3.6 us -> none  [product(): jnp.einsum('cij,cjr->cir', mats, vals, preferred_element_type=jnp.float32)]
  transfers between devices with their start and end apart: 1 -> 0, of which waited for: 1 -> 0; matrix products, arithmetic and copies ran while one was open for 0% -> 0% of each run, Pallas kernels for 0% -> 0%
where the time goes in v2:
time: 52.6 us
  Pallas kernels  51.9 us (99%)
  between operations  0.66 us (1%)
    pallas_call x1, Pallas kernels, on_device(): pl.pallas_call(forward_kernel, out_shape=(jax.ShapeDtypeStruct((256, 32,...  49.5 us
    pallas_call x1, Pallas kernels, on_device(): pl.pallas_call(backward_kernel, out_shape=(jax.ShapeDtypeStruct(child_rhs...  2.42 us

profile of v2, /device:TPU:1, one launch (start us, length us, event | category | flops | bytes accessed | tf_op | source)
XLA Modules:
  0.0 52.6 jit_solution(17637902545518521900)
XLA Ops:
  0.6 0.0 copy-start
  0.6 49.5 %shard_map.104 = (bf16[256,32,128]{2,1,0:T(8,128)(2,1)S(1)}, f32[48,128,128]{2,1,0:T(8,128)S(1)}, bf16[48,128,128]{2,1,0:T(8,128)(2,1)S(1)}) custom-call(s32[1,48]{1,0:T(1,128)} %bitcast.1, bf16[48,128,128]{2,1,0:T(8,128)(2,1)} %rhs_h.1, bf16[1,128,128]{2,1,0:T(8,128)(2,1)} %prhs_h.1, bf16[48,128,128]{2,1,0:T(8,128)(2,1)} %linv_h.1, ...), custom_call_target="tpu_custom_call" | custom-call | tf_op jit(solution)/shard_map/pallas_call | solution.py:416
  50.1 0.0 copy-done
  50.1 2.4 %shard_map.105 = (bf16[48,128,128]{2,1,0:T(8,128)(2,1)}, bf16[1,128,128]{2,1,0:T(8,128)(2,1)}) custom-call(s32[48]{0:T(128)S(1)} %copy-done, bf16[256,32,128]{2,1,0:T(8,128)(2,1)S(1)} %get-tuple-element.5.gath, f32[48,128,128]{2,1,0:T(8,128)S(1)} %get-tuple-element.6.ufwd, bf16[48,128,128]{2,1,0:T(8,128)(2,1)S(1)} %get-tuple-element.7.mat), custom_call_target="tpu_custom_call" | custom-call | tf_op jit(solution)/shard_map/pallas_call | solution.py:474
Async XLA Ops:
  0.6 49.5 %copy-start = (s32[48]{0:T(128)S(1)}, s32[48]{0:T(128)}, u32[]{:S(2)}) copy-start(s32[48]{0:T(128)} %po.1) | copy-start | bytes 580

commit v3 on v2

--- a/solution.py
+++ b/solution.py
@@ -59,7 +59,6 @@
     sib,
     sibr,
     snd,
-    r1,
     fin,
     snd2,
     gin,
@@ -151,11 +150,10 @@
             c = k * GRP + j
             run[c] = terms[j] + run[tab[0, c]]
 
-    def mine_of(t, i, h, n, core_):
-        b_, zz = h * 2 + lax.div(n, 4), t * 4 + lax.rem(n, 4)
-        x_, y_ = (i, b_) if t == 0 else (b_, i)
+    def mine_of(t, b_, a_, zz, core_):
+        x_, y_ = (a_, b_) if t == 0 else (b_, a_)
         row = pl.multiple_of(x_ * 32, 32)
-        last_ = tab[0, 64 + y_ * 16 + zz * 2 + core_]
+        last_ = tab[0, 64 + y_ * 16 + (t * 4 + zz) * 2 + core_]
         return run[last_, pl.ds(row, 32), :]
 
     def remote(src, dst, slot, dev_):
@@ -183,93 +181,62 @@
     def slot(*key):
         return slots.setdefault(key, len(slots))
 
-    def half(i, h):
-        return pl.ds(i * 16 + h * 8, 8)
-
     both = (0, 1)
-    order = [(2, 0), (2, 1), (1, 1), (3, 0), (1, 0), (3, 1), (0, 0), (0, 1)]
-
-    for s, (d, h) in enumerate(order):
-        for t in both:
-            i = ax[t][d]
-
-            def pack(n, t=t, i=i, h=h):
-                u = i * 16 + h * 8 + n
-                sib[t, u] = mine_of(t, i, h, n, flip).astype(BF)
-
-            loop(8, pack, unroll=8)
-            if s == 0 and t == 0:
+    order = (2, 1, 3, 0)
+
+    def row_of(b_):
+        return pl.ds(b_ * 16, 16)
+
+    waited = False
+    for d in order:
+        for t in both:
+            b_ = bx[t][d]
+            for a_ in range(4):
+                for zz in range(4):
+                    v = mine_of(t, b_, a_, zz, flip)
+                    sib[t, b_ * 16 + a_ * 4 + zz] = v.astype(BF)
+            if not waited:
                 pl.semaphore_wait(barrier, len(peers))
-            send(
-                sib.at[t, half(i, h)], sibr.at[t, half(i, h)], slot("s0", t, s), d_sib
-            )
-
-    def from_sib(t, s):
-        d, h = order[s]
-        arrived(sibr.at[t, half(ax[t][d], h)], slot("s0", t, s))
-
-    def joined(t, d, h, more=None):
-        i = ax[t][d]
-
-        def body(n):
-            u = i * 16 + h * 8 + n
-            v = mine_of(t, i, h, n, core) + sibr[t, u].astype(F32)
-            if more is not None:
-                v = v + more[n].astype(F32)
-            snd[t, u] = v.astype(BF)
-
-        loop(8, body, unroll=8)
-        return snd.at[t, half(i, h)]
-
-    H = [pl.ds(0, 8), pl.ds(8, 8)]
-    for t in both:
-        from_sib(t, 0)
-        send(joined(t, 2, 0), r1.at[t, 0], slot("r1", t, 0), d_a[t][1])
-        from_sib(t, 1)
-        send(joined(t, 2, 1), r1.at[t, 1], slot("r1", t, 1), d_a[t][3])
-    for t in both:
-        from_sib(t, 2)
-        send(joined(t, 1, 1), fin.at[t, 0, H[1]], slot("f", t, 0, 1), d_a[t][1])
-        from_sib(t, 3)
-        send(joined(t, 3, 0), fin.at[t, 1, H[0]], slot("f", t, 1, 0), d_a[t][3])
-    for t in both:
-        for s in (4, 5):
-            from_sib(t, s)
-    for t in both:
-        arrived(r1.at[t, 0], slot("r1", t, 0))
-        src = joined(t, 1, 0, r1.at[t, 0])
-        send(src, fin.at[t, 0, H[0]], slot("f", t, 0, 0), d_a[t][1])
-        arrived(r1.at[t, 1], slot("r1", t, 1))
-        src = joined(t, 3, 1, r1.at[t, 1])
-        send(src, fin.at[t, 1, H[1]], slot("f", t, 1, 1), d_a[t][3])
-    for t in both:
-        for s in (6, 7):
-            from_sib(t, s)
-    for t in both:
-        arrived(fin.at[t, 0, H[1]], slot("f", t, 0, 1))
-        arrived(fin.at[t, 1, H[0]], slot("f", t, 1, 0))
-
-    def at_a(t, b_, zz):
-        n = b_ * 4 + zz
-        v = mine_of(t, ax[t][0], 0, n, core) + sibr[t, ax[t][0] * 16 + n].astype(F32)
-        return v + fin[t, 0, n].astype(F32) + fin[t, 1, n].astype(F32)
-
-    for t in both:
-        arrived(fin.at[t, 0, H[0]], slot("f", t, 0, 0))
-        arrived(fin.at[t, 1, H[1]], slot("f", t, 1, 1))
-        for d in (2, 1, 3):
+                waited = True
+            rows_ = row_of(b_)
+            send(sib.at[t, rows_], sibr.at[t, rows_], slot("s0", t, d), d_sib)
+
+    for e in order:
+        for t in both:
+            b_ = bx[t][e]
+            arrived(sibr.at[t, row_of(b_)], slot("s0", t, e))
+            for d in order[:3]:
+                a_ = ax[t][d]
+                for zz in range(4):
+                    u = b_ * 16 + a_ * 4 + zz
+                    v = mine_of(t, b_, a_, zz, core) + sibr[t, u].astype(F32)
+                    snd[t, u] = v.astype(BF)
+                src = snd.at[t, pl.ds(b_ * 16 + a_ * 4, 4)]
+                send(src, fin.at[t, d - 1, e], slot("f", t, d, e), d_a[t][d])
+
+    def at_a(t, e, zz):
+        b_, a_ = bx[t][e], ax[t][0]
+        v = mine_of(t, b_, a_, zz, core) + sibr[t, b_ * 16 + a_ * 4 + zz].astype(F32)
+        for d in range(3):
+            v = v + fin[t, d, e, zz].astype(F32)
+        return v
+
+    for e in order:
+        for t in both:
+            for d in order[:3]:
+                arrived(fin.at[t, d - 1, e], slot("f", t, d, e))
+            if e == 0:
+                continue
             for zz in range(4):
-                snd2[t, d - 1, zz] = at_a(t, bx[t][d], zz).astype(BF)
-            send(snd2.at[t, d - 1], gin.at[t, d - 1], slot("g", t, d), d_b[t][d])
+                snd2[t, e - 1, zz] = at_a(t, e, zz).astype(BF)
+            send(snd2.at[t, e - 1], gin.at[t, e - 1], slot("g", t, e), d_b[t][e])
 
     def at_b(t, zz):
-        v = at_a(t, bx[t][0], zz)
+        v = at_a(t, 0, zz)
         for d in range(3):
             v = v + gin[t, d, zz].astype(F32)
         return v
 
-    near = lax.div(z, 4)
-    tot = []
     for t in both:
         for d in (2, 1, 3):
             arrived(gin.at[t, d - 1], slot("g", t, d))
@@ -304,7 +271,7 @@
 
     def unit(z_):
         t_ = lax.div(z_, 4)
-        ab = (1 - t_) * (x * 4 + y) + t_ * (y * 4 + x)
+        ab = (1 - t_) * (y * 4 + x) + t_ * (x * 4 + y)
         return (core * 2 + t_) * 64 + ab * 4 + lax.rem(z_, 4)
 
     me = unit(z)
@@ -318,52 +285,34 @@
     def share(ref_slice, slot_, dev_):
         send(gath.at[ref_slice], gath.at[ref_slice], slot_, dev_)
 
-    def bsl(t, d):
-        return pl.ds((core * 2 + t) * 64 + ax[t][0] * 16 + bx[t][d] * 4, 4)
+    def piece(t, e, d, core_=core):
+        return pl.ds((core_ * 2 + t) * 64 + bx[t][e] * 16 + ax[t][d] * 4, 4)
+
+    def whole_row(t, e, core_=core):
+        return pl.ds((core_ * 2 + t) * 64 + bx[t][e] * 16, 16)
+
+    def along_a(t, e):
+        for d in order[:3]:
+            share(piece(t, e, 0), slot("ba", t, e, d), d_a[t][d])
 
     for t in both:
-        for d in (2, 1, 3):
-            share(bsl(t, 0), slot("bb", t, d), d_b[t][d])
-    for d in (1, 3, 2):
-        for t in both:
-            arrived(gath.at[bsl(t, 4 - d)], slot("bb", t, d))
-
-    def asl(t, d, h, core_=core):
-        return pl.ds((core_ * 2 + t) * 64 + ax[t][d] * 16 + h * 8, 8)
-
-    def over(t, d, h):
-        share(asl(t, d, h), slot("o", t, d, h), d_sib)
-
+        for e in order[:3]:
+            share(piece(t, 0, 0), slot("bb", t, e), d_b[t][e])
     for t in both:
-        share(asl(t, 0, 0), slot("ba", t, 1, 0), d_a[t][1])
-        share(asl(t, 0, 1), slot("ba", t, 3, 1), d_a[t][3])
-    for t in both:
-        share(asl(t, 0, 1), slot("ba", t, 1, 1), d_a[t][1])
-        share(asl(t, 0, 0), slot("ba", t, 3, 0), d_a[t][3])
-    for t in both:
-        for h in (0, 1):
-            over(t, 0, h)
-    for t in both:
-        arrived(gath.at[asl(t, 3, 0)], slot("ba", t, 1, 0))
-        share(asl(t, 3, 0), slot("ba", t, 2, 0), d_a[t][1])
-        arrived(gath.at[asl(t, 1, 1)], slot("ba", t, 3, 1))
-        share(asl(t, 1, 1), slot("ba", t, 2, 1), d_a[t][3])
-    for t in both:
-        over(t, 3, 0)
-        over(t, 1, 1)
-    for t in both:
-        arrived(gath.at[asl(t, 3, 1)], slot("ba", t, 1, 1))
-        over(t, 3, 1)
-        arrived(gath.at[asl(t, 1, 0)], slot("ba", t, 3, 0))
-        over(t, 1, 0)
-    for h in (0, 1):
-        for t in both:
-            arrived(gath.at[asl(t, 2, h)], slot("ba", t, 2, h))
-            over(t, 2, h)
-    for d in (0, 3, 1, 2):
-        for h in (0, 1):
-            for t in both:
-                arrived(gath.at[asl(t, d, h, flip)], slot("o", t, d, h))
+        along_a(t, 0)
+    for e in (1, 3, 2):
+        for t in both:
+            arrived(gath.at[piece(t, e, 0)], slot("bb", t, 4 - e))
+            along_a(t, e)
+    back = (0, 1, 3, 2)
+    for e in back:
+        for t in both:
+            for d in back[1:]:
+                arrived(gath.at[piece(t, e, d)], slot("ba", t, e, 4 - d))
+            share(whole_row(t, e), slot("o", t, e), d_sib)
+    for e in back:
+        for t in both:
+            arrived(gath.at[whole_row(t, e, flip)], slot("o", t, e))
     for cp in sends:
         cp.wait_send()
 
@@ -371,8 +320,8 @@
 def parent_of_units(gath, p):
     h, z, y = lax.rem(p, 2), lax.rem(lax.div(p, 2), 8), lax.div(p, 16)
     t = lax.div(z, 4)
-    first = (h * 2 + t) * 64 + lax.rem(z, 4) + (1 - t) * y * 4 + t * y * 16
-    stride = (1 - t) * 16 + t * 4
+    first = (h * 2 + t) * 64 + lax.rem(z, 4) + (1 - t) * y * 16 + t * y * 4
+    stride = (1 - t) * 4 + t * 16
     return jnp.concatenate([gath[first + q * stride] for q in range(4)], axis=0)
 
 
@@ -439,8 +388,7 @@
             units(2, 64),
             units(2, 64),
             units(2, 64),
-            units(2, 2, 8),
-            units(2, 2, 16),
+            units(2, 3, 4, 4),
             units(2, 3, 4),
             units(2, 3, 4),
             pltpu.VMEM((8, 32, 128), F32),

time: 52.6 us -> 48.4 us (0.920)
  Pallas kernels: 51.9 us -> 47.6 us
    pallas_call x1, Pallas kernels: 49.5 us -> 45.2 us  [on_device(): pl.pallas_call(forward_kernel, out_shape=(jax.ShapeDtypeStruct((256, 32,...]
where the time goes in v3:
time: 48.4 us; the launch traced here: 48.3 us
  Pallas kernels  47.6 us (98%)
  between operations  0.66 us (1%)
    pallas_call x1, Pallas kernels, on_device(): pl.pallas_call(forward_kernel, out_shape=(jax.ShapeDtypeStruct((256, 32,...  45.2 us
    pallas_call x1, Pallas kernels, on_device(): pl.pallas_call(backward_kernel, out_shape=(jax.ShapeDtypeStruct(child_rhs...  2.42 us

profile of v3, /device:TPU:1, one launch (start us, length us, event | category | flops | bytes accessed | tf_op | source)
XLA Modules:
  0.0 48.3 jit_solution(9470714662882370834)
XLA Ops:
  0.6 0.0 copy-start
  0.6 45.2 %shard_map.104 = (bf16[256,32,128]{2,1,0:T(8,128)(2,1)S(1)}, f32[48,128,128]{2,1,0:T(8,128)S(1)}, bf16[48,128,128]{2,1,0:T(8,128)(2,1)S(1)}) custom-call(s32[1,48]{1,0:T(1,128)} %bitcast.1, bf16[48,128,128]{2,1,0:T(8,128)(2,1)} %rhs_h.1, bf16[1,128,128]{2,1,0:T(8,128)(2,1)} %prhs_h.1, bf16[48,128,128]{2,1,0:T(8,128)(2,1)} %linv_h.1, ...), custom_call_target="tpu_custom_call" | custom-call | tf_op jit(solution)/shard_map/pallas_call | solution.py:365
  45.8 0.0 copy-done
  45.9 2.4 %shard_map.105 = (bf16[48,128,128]{2,1,0:T(8,128)(2,1)}, bf16[1,128,128]{2,1,0:T(8,128)(2,1)}) custom-call(s32[48]{0:T(128)S(1)} %copy-done, bf16[256,32,128]{2,1,0:T(8,128)(2,1)S(1)} %get-tuple-element.5.gath, f32[48,128,128]{2,1,0:T(8,128)S(1)} %get-tuple-element.6.ufwd, bf16[48,128,128]{2,1,0:T(8,128)(2,1)S(1)} %get-tuple-element.7.mat), custom_call_target="tpu_custom_call" | custom-call | tf_op jit(solution)/shard_map/pallas_call | solution.py:422
Async XLA Ops:
  0.6 45.2 %copy-start = (s32[48]{0:T(128)S(1)}, s32[48]{0:T(128)}, u32[]{:S(2)}) copy-start(s32[48]{0:T(128)} %po.1) | copy-start | bytes 580

commit v4 on v3

v4 whole, which is shorter than its diff:
```python
import jax
import jax.numpy as jnp
from jax import lax
from jax.experimental import pallas as pl
from jax.experimental.pallas import tpu as pltpu
from jax.sharding import PartitionSpec as P

BF = jnp.bfloat16
F32 = jnp.float32
MESH = pl.DeviceIdType.MESH
NCH = 48
GRP = 8
CHUNKS = NCH // GRP
NT = (((1,), (1,)), ((), ()))


def mm(a, b):
    return jnp.dot(a, b, preferred_element_type=F32)


def mm_nt(a, b):
    return lax.dot_general(a, b, NT, preferred_element_type=F32)


def loop(n, body, unroll=1):
    def step(i, carry):
        body(i)
        return carry

    lax.fori_loop(0, n, step, 0, unroll=unroll)


NEAR = (0, 1, 7, 2, 6, 3, 5, 4)
PARTS = range(4)


def place_of(p, z):
    h, pz, y = lax.rem(p, 2), lax.rem(lax.div(p, 2), 8), lax.div(p, 16)
    far = lax.rem(pz - z + 8, 8)
    pos = jnp.maximum(jnp.minimum(2 * far - 1, 16 - 2 * far), 0)
    t, odd = lax.div(pos, 2), lax.rem(lax.div(pos, 2), 2)
    first = (h * 4 + t) * 32 + lax.rem(pos, 2) + (1 - odd) * y * 8 + odd * y * 2
    return first, (1 - odd) * 2 + odd * 8


def parent_of_units(gath, p, z):
    first, step = place_of(p, z)
    return jnp.concatenate([gath[first + q * step] for q in range(4)], axis=0)


def forward_kernel(
    po_h,
    rhs_h,
    prhs_h,
    linv_h,
    loff_h,
    uinv_h,
    uoff_h,
    plinv_h,
    puinv_h,
    gath,
    ufwd,
    mat,
    rhs,
    linv,
    loff,
    uinv,
    uoff,
    prhs,
    plinv,
    puinv,
    fwd,
    run,
    pov,
    tabv,
    tab,
    sib,
    sibr,
    snd,
    fin,
    snd2,
    gin,
    held,
    zr_out,
    zr,
    sol,
    prt,
    load_sem,
    tab_sem,
    send_sem,
    recv_sem,
):
    x = lax.axis_index("row")
    col = lax.axis_index("col")
    core = lax.rem(col, 2)
    z = lax.rem(lax.div(col, 2), 8)
    y = lax.div(col, 16)
    flip = 1 - core

    def dev(x_, y_, z_, c_):
        return (x_, y_ * 16 + z_ * 2 + c_)

    def mod4(v):
        return lax.rem(v, 4)

    d_sib = dev(x, y, z, flip)
    d_x = [dev(mod4(x + d), y, z, core) for d in range(4)]
    d_y = [dev(x, mod4(y + d), z, core) for d in range(4)]
    zs = [lax.rem(z + d, 8) for d in range(8)]
    d_z = [dev(x, y, zs[d], core) for d in range(8)]
    d_a, d_b = (d_x, d_y) * 2, (d_y, d_x) * 2
    x_at, y_at = [mod4(x + d) for d in range(4)], [mod4(y + d) for d in range(4)]
    ax, bx = (x_at, y_at) * 2, (y_at, x_at) * 2

    loads, sends, pend = [], [], {}

    def load(src, dst):
        cp = pltpu.make_async_copy(src, dst, load_sem.at[len(loads)])
        cp.start()
        loads.append(cp)
        return cp

    starts = [0, 4] + list(range(8, NCH + 1, GRP))
    spans = list(zip(starts[:-1], starts[1:], strict=True))

    def load_span(lo, hi):
        part = pl.ds(lo, hi - lo)
        pairs = ((linv_h, linv), (rhs_h, rhs), (loff_h, loff))
        return [load(src.at[part], dst.at[part]) for src, dst in pairs]

    span_loads = [load_span(*spans[0])]
    po_load = load(po_h, pov)
    span_loads += [load_span(*span) for span in spans[1:]]

    barrier = pltpu.get_barrier_semaphore()
    peers = [d_sib] + d_x[1:] + d_y[1:] + d_z[1:]
    for peer in peers:
        pl.semaphore_signal(barrier, inc=1, device_id=peer, device_id_type=MESH)

    run[NCH] = jnp.zeros((128, 128), F32)

    def table():
        po_load.wait()
        mine = jnp.concatenate(
            [pov[...], jnp.full((1, 128 - NCH), -1, jnp.int32)], axis=1
        )
        rows = jnp.broadcast_to(mine, (128, 128))
        lane = lax.broadcasted_iota(jnp.int32, (128, 128), 1)
        child = lax.broadcasted_iota(jnp.int32, (128, 128), 0)
        label = jnp.where(lane < 64, rows, lane - 64)
        hit = (rows.T == label) & (child < jnp.where(lane < 64, lane, NCH))
        last = jnp.max(jnp.where(hit, child, -1), axis=0, keepdims=True)
        tabv[...] = jnp.where(last < 0, NCH, last)
        cp = pltpu.make_async_copy(tabv, tab, tab_sem.at[0])
        cp.start()
        return cp

    for k, (lo, hi) in enumerate(spans):
        for cp in span_loads[k]:
            cp.wait()
        terms = []
        for c in range(lo, hi):
            f = mm(linv[c], rhs[c]).astype(BF)
            fwd[c] = f
            term = mm_nt(f.T, loff[c])
            if k < 2:
                run[c] = term
            terms.append(term)
        if k == 0:
            tab_copy = table()
        elif k == 1:
            upper_loads = [load(uinv_h, uinv), load(uoff_h, uoff)]
            parent_loads = [
                load(prhs_h, prhs),
                load(plinv_h, plinv),
                load(puinv_h, puinv),
            ]
            tab_copy.wait()
            for c in range(hi):
                run[c] = run[c] + run[tab[0, c]]
        else:
            for c in range(lo, hi):
                run[c] = terms[c - lo] + run[tab[0, c]]

    def mine_of(t, b_, a_, zz, core_):
        x_, y_ = (b_, a_) if t % 2 else (a_, b_)
        row = pl.multiple_of(x_ * 32, 32)
        last_ = tab[0, 64 + y_ * 16 + zs[NEAR[t * 2 + zz]] * 2 + core_]
        return run[last_, pl.ds(row, 32), :]

    def remote(src, dst, slot, dev_):
        return pltpu.make_async_remote_copy(
            src_ref=src,
            dst_ref=dst,
            send_sem=send_sem.at[slot],
            recv_sem=recv_sem.at[slot],
            device_id=dev_,
            device_id_type=MESH,
        )

    def send(src, dst, slot, dev_):
        cp = remote(src, dst, slot, dev_)
        cp.start()
        sends.append(cp)
        pend[slot] = src

    def arrived(dst, slot):
        remote(dst, dst, slot, d_sib).wait_recv()
        pend.pop(slot)

    slots = {}

    def slot(*key):
        return slots.setdefault(key, len(slots))

    order = (2, 1, 3, 0)
    far_first = (3, 2, 1, 0)

    def row_of(b_):
        return pl.ds(b_ * 8, 8)

    waited = False
    for e in order:
        for t in far_first:
            b_ = bx[t][e]
            for a_ in range(4):
                for zz in range(2):
                    v = mine_of(t, b_, a_, zz, flip)
                    sib[t, b_ * 8 + a_ * 2 + zz] = v.astype(BF)
            if not waited:
                pl.semaphore_wait(barrier, len(peers))
                waited = True
            rows_ = row_of(b_)
            send(sib.at[t, rows_], sibr.at[t, rows_], slot("s0", t, e), d_sib)

    for e in order:
        for t in far_first:
            b_ = bx[t][e]
            arrived(sibr.at[t, row_of(b_)], slot("s0", t, e))
            for d in order[:3]:
                a_ = ax[t][d]
                for zz in range(2):
                    u = b_ * 8 + a_ * 2 + zz
                    v = mine_of(t, b_, a_, zz, core) + sibr[t, u].astype(F32)
                    snd[t, u] = v.astype(BF)
                src = snd.at[t, pl.ds(b_ * 8 + a_ * 2, 2)]
                send(src, fin.at[t, d - 1, e], slot("f", t, d, e), d_a[t][d])

    def at_a(t, e, zz):
        b_, a_ = bx[t][e], ax[t][0]
        v = mine_of(t, b_, a_, zz, core) + sibr[t, b_ * 8 + a_ * 2 + zz].astype(F32)
        for d in range(3):
            v = v + fin[t, d, e, zz].astype(F32)
        return v

    for e in order:
        for t in far_first:
            for d in order[:3]:
                arrived(fin.at[t, d - 1, e], slot("f", t, d, e))
            for zz in range(2):
                v = at_a(t, e, zz)
                if e == 0:
                    held[t * 2 + zz] = v
                else:
                    snd2[t, e - 1, zz] = v.astype(BF)
            if e:
                send(snd2.at[t, e - 1], gin.at[t, e - 1], slot("g", t, e), d_b[t][e])

    for t in far_first:
        for e in order[:3]:
            arrived(gin.at[t, e - 1], slot("g", t, e))
        for zz in (1, 0):
            pos = t * 2 + zz
            v = held[pos]
            for e in range(3):
                v = v + gin[t, e, zz].astype(F32)
            if pos == 0:
                total = v
                continue
            d = NEAR[pos]
            zr_out[d - 1] = v.astype(BF)
            send(zr_out.at[d - 1], zr.at[d - 1], slot("z", d), d_z[d])
    held[0] = total

    for cp in parent_loads:
        cp.wait()
    prt[...] = prhs[0].astype(F32).T
    for cp in upper_loads:
        cp.wait()

    def prepare(i):
        for j in range(4):
            c = i * 4 + j
            ui = uinv[c]
            ufwd[c] = mm(ui, fwd[c])
            mat[c] = mm(ui, uoff[c]).astype(BF)

    loop(NCH // 4, prepare)

    total = held[0]
    for d in range(1, 8):
        arrived(zr.at[d - 1], slot("z", d))
        total = total + zr[d - 1].astype(F32)

    res = (prt[pl.ds(pl.multiple_of(x * 32, 32), 32), :] - total).astype(BF)
    pf = mm_nt(res, plinv[0]).astype(BF)

    def unit(pos):
        t = pos // 2
        return (core * 4 + t) * 32 + bx[t][0] * 8 + ax[t][0] * 2 + pos % 2

    sol[...] = mm_nt(pf, puinv[0]).astype(BF)
    gath[unit(0)] = sol[...]

    for d in (4, 3, 5, 2, 6, 1, 7):
        dst = gath.at[unit(NEAR.index(8 - d))]
        send(sol, dst, slot("bz", d), d_z[d])

    def share(ref_slice, slot_, dev_):
        send(gath.at[ref_slice], gath.at[ref_slice], slot_, dev_)

    def piece(t, e, d, core_=core):
        return pl.ds((core_ * 4 + t) * 32 + bx[t][e] * 8 + ax[t][d] * 2, 2)

    def whole_row(t, e, core_=core):
        return pl.ds((core_ * 4 + t) * 32 + bx[t][e] * 8, 8)

    def along_a(t, e):
        for d in order[:3]:
            share(piece(t, e, 0), slot("ba", t, e, d), d_a[t][d])

    def along_b(t):
        for pos in (t * 2, t * 2 + 1):
            if pos:
                arrived(gath.at[unit(pos)], slot("bz", 8 - NEAR[pos]))
        for e in order[:3]:
            share(piece(t, 0, 0), slot("bb", t, e), d_b[t][e])
        along_a(t, 0)

    def along_row(t, e):
        arrived(gath.at[piece(t, e, 0)], slot("bb", t, 4 - e))
        along_a(t, e)

    def across(t, e):
        for d in (1, 3, 2):
            arrived(gath.at[piece(t, e, d)], slot("ba", t, e, 4 - d))
        share(whole_row(t, e), slot("o", t, e), d_sib)

    for t in PARTS:
        along_b(t)
    for t in (0, 1):
        for e in (1, 3, 2):
            along_row(t, e)
    for t in (0, 1):
        across(t, 0)
    for t in (2, 3):
        for e in (1, 3, 2):
            along_row(t, e)
    for t in (0, 1):
        for e in (1, 3, 2):
            across(t, e)
    for e in (0, 1, 3, 2):
        for t in (2, 3):
            across(t, e)
    for t in PARTS:
        for e in (0, 1, 3, 2):
            arrived(gath.at[whole_row(t, e, flip)], slot("o", t, e))
    for cp in sends:
        cp.wait_send()


def backward_kernel(po, gath, ufwd, mat, out_h, psol_h, out, psol, sem):
    col = lax.axis_index("col")
    z = lax.rem(lax.div(col, 2), 8)
    psol[0] = parent_of_units(gath, col, z).T
    copies = []

    def put(src, dst):
        cp = pltpu.make_async_copy(src, dst, sem.at[len(copies)])
        cp.start()
        copies.append(cp)

    put(psol, psol_h)
    for k in range(CHUNKS):
        for c in range(k * GRP, (k + 1) * GRP):
            s = parent_of_units(gath, po[c], z)
            out[c] = (ufwd[c] - mm_nt(mat[c], s)).astype(BF)
        part = pl.ds(k * GRP, GRP)
        put(out.at[part], out_h.at[part])
    for cp in copies:
        cp.wait()


def on_device(
    child_rhs,
    parent_rhs,
    child_lower_inv,
    child_lower_off,
    child_upper_inv,
    child_upper_off,
    parent_lower_inv,
    parent_upper_inv,
    parent_of,
):
    mats = lambda: pltpu.VMEM((NCH, 128, 128), BF)
    one = lambda: pltpu.VMEM((1, 128, 128), BF)
    units = lambda *k: pltpu.VMEM((*k, 32, 128), BF)
    smem = pl.BlockSpec(memory_space=pltpu.SMEM)
    vmem = pl.BlockSpec(memory_space=pltpu.VMEM)
    hbm = pl.BlockSpec(memory_space=pl.ANY)
    gath, ufwd, mat = pl.pallas_call(
        forward_kernel,
        out_shape=(
            jax.ShapeDtypeStruct((256, 32, 128), BF),
            jax.ShapeDtypeStruct((NCH, 128, 128), F32),
            jax.ShapeDtypeStruct((NCH, 128, 128), BF),
        ),
        in_specs=[hbm] * 9,
        out_specs=(vmem, vmem, vmem),
        scratch_shapes=[
            mats(),
            mats(),
            mats(),
            mats(),
            mats(),
            one(),
            one(),
            one(),
            mats(),
            pltpu.VMEM((NCH + 1, 128, 128), F32),
            pltpu.VMEM((1, NCH), jnp.int32),
            pltpu.VMEM((1, 128), jnp.int32),
            pltpu.SMEM((1, 128), jnp.int32),
            units(4, 32),
            units(4, 32),
            units(4, 32),
            units(4, 3, 4, 2),
            units(4, 3, 2),
            units(4, 3, 2),
            pltpu.VMEM((8, 32, 128), F32),
            units(7),
            units(7),
            units(),
            pltpu.VMEM((128, 128), F32),
            pltpu.SemaphoreType.DMA((3 * CHUNKS + 9,)),
            pltpu.SemaphoreType.DMA((1,)),
            pltpu.SemaphoreType.DMA((166,)),
            pltpu.SemaphoreType.DMA((166,)),
        ],
        compiler_params=pltpu.CompilerParams(
            collective_id=0, has_side_effects=True, vmem_limit_bytes=40 * 2**20
        ),
    )(
        *[
            pltpu.with_memory_space_constraint(v, pltpu.HBM)
            for v in (
                parent_of.reshape(1, NCH),
                child_rhs,
                parent_rhs,
                child_lower_inv,
                child_lower_off,
                child_upper_inv,
                child_upper_off,
                parent_lower_inv,
                parent_upper_inv,
            )
        ]
    )
    return pl.pallas_call(
        backward_kernel,
        out_shape=(
            jax.ShapeDtypeStruct(child_rhs.shape, BF),
            jax.ShapeDtypeStruct(parent_rhs.shape, BF),
        ),
        in_specs=[smem, vmem, vmem, vmem],
        out_specs=(hbm, hbm),
        scratch_shapes=[mats(), one(), pltpu.SemaphoreType.DMA((CHUNKS + 1,))],
        compiler_params=pltpu.CompilerParams(vmem_limit_bytes=16 * 2**20),
    )(parent_of, gath, ufwd, mat)


def solution(mesh):
    child = P(("row", "col"), None, None)
    par = P("col", None, None)
    return jax.shard_map(
        on_device,
        mesh=mesh,
        in_specs=(child, par, child, child, child, child, par, par, P(("row", "col"))),
        out_specs=(child, par),
        check_vma=False,
    )
```

time: 48.4 us -> 48.4 us (level)
  no operation moved by 1% of the time
where the time goes in v4:
time: 48.4 us; the launch traced here: 48.3 us
  Pallas kernels  47.7 us (99%)
  between operations  0.66 us (1%)
    pallas_call x1, Pallas kernels, on_device(): pl.pallas_call(forward_kernel, out_shape=(jax.ShapeDtypeStruct((256, 32,...  45.2 us
    pallas_call x1, Pallas kernels, on_device(): pl.pallas_call(backward_kernel, out_shape=(jax.ShapeDtypeStruct(child_rhs...  2.46 us

profile of v4, /device:TPU:1, one launch (start us, length us, event | category | flops | bytes accessed | tf_op | source)
XLA Modules:
  0.0 48.3 jit_solution(11121765375636896602)
XLA Ops:
  0.6 0.0 copy-start
  0.6 45.2 %shard_map.104 = (bf16[256,32,128]{2,1,0:T(8,128)(2,1)S(1)}, f32[48,128,128]{2,1,0:T(8,128)S(1)}, bf16[48,128,128]{2,1,0:T(8,128)(2,1)S(1)}) custom-call(s32[1,48]{1,0:T(1,128)} %bitcast.1, bf16[48,128,128]{2,1,0:T(8,128)(2,1)} %rhs_h.1, bf16[1,128,128]{2,1,0:T(8,128)(2,1)} %prhs_h.1, bf16[48,128,128]{2,1,0:T(8,128)(2,1)} %linv_h.1, ...), custom_call_target="tpu_custom_call" | custom-call | tf_op jit(solution)/shard_map/pallas_call | solution.py:411
  45.9 0.0 copy-done
  45.9 2.5 %shard_map.105 = (bf16[48,128,128]{2,1,0:T(8,128)(2,1)}, bf16[1,128,128]{2,1,0:T(8,128)(2,1)}) custom-call(s32[48]{0:T(128)S(1)} %copy-done, bf16[256,32,128]{2,1,0:T(8,128)(2,1)S(1)} %get-tuple-element.5.gath, f32[48,128,128]{2,1,0:T(8,128)S(1)} %get-tuple-element.6.ufwd, bf16[48,128,128]{2,1,0:T(8,128)(2,1)S(1)} %get-tuple-element.7.mat), custom_call_target="tpu_custom_call" | custom-call | tf_op jit(solution)/shard_map/pallas_call | solution.py:469
Async XLA Ops:
  0.6 45.2 %copy-start = (s32[48]{0:T(128)S(1)}, s32[48]{0:T(128)}, u32[]{:S(2)}) copy-start(s32[48]{0:T(128)} %po.1) | copy-start | bytes 580

commit v5 on v4

--- a/solution.py
+++ b/solution.py
@@ -128,9 +128,10 @@
         pairs = ((linv_h, linv), (rhs_h, rhs), (loff_h, loff))
         return [load(src.at[part], dst.at[part]) for src, dst in pairs]
 
-    span_loads = [load_span(*spans[0])]
     po_load = load(po_h, pov)
-    span_loads += [load_span(*span) for span in spans[1:]]
+    span_loads = [load_span(*span) for span in spans]
+    upper_loads = [load(uinv_h, uinv), load(uoff_h, uoff)]
+    parent_loads = [load(prhs_h, prhs), load(plinv_h, plinv), load(puinv_h, puinv)]
 
     barrier = pltpu.get_barrier_semaphore()
     peers = [d_sib] + d_x[1:] + d_y[1:] + d_z[1:]
@@ -155,6 +156,7 @@
         cp.start()
         return cp
 
+    tab_copy = table()
     for k, (lo, hi) in enumerate(spans):
         for cp in span_loads[k]:
             cp.wait()
@@ -166,19 +168,11 @@
             if k < 2:
                 run[c] = term
             terms.append(term)
-        if k == 0:
-            tab_copy = table()
-        elif k == 1:
-            upper_loads = [load(uinv_h, uinv), load(uoff_h, uoff)]
-            parent_loads = [
-                load(prhs_h, prhs),
-                load(plinv_h, plinv),
-                load(puinv_h, puinv),
-            ]
+        if k == 1:
             tab_copy.wait()
             for c in range(hi):
                 run[c] = run[c] + run[tab[0, c]]
-        else:
+        elif k > 1:
             for c in range(lo, hi):
                 run[c] = terms[c - lo] + run[tab[0, c]]
 

time: 48.4 us -> 48.4 us (level)
  no operation moved by 1% of the time
where the time goes in v5:
time: 48.4 us; the launch traced here: 48.3 us
  Pallas kernels  47.6 us (98%)
  between operations  0.66 us (1%)
    pallas_call x1, Pallas kernels, on_device(): pl.pallas_call(forward_kernel, out_shape=(jax.ShapeDtypeStruct((256, 32,...  45.1 us
    pallas_call x1, Pallas kernels, on_device(): pl.pallas_call(backward_kernel, out_shape=(jax.ShapeDtypeStruct(child_rhs...  2.47 us

profile of v5, /device:TPU:1, one launch (start us, length us, event | category | flops | bytes accessed | tf_op | source)
XLA Modules:
  0.0 48.3 jit_solution(9364677384154585339)
XLA Ops:
  0.6 0.0 copy-start
  0.6 45.1 %shard_map.104 = (bf16[256,32,128]{2,1,0:T(8,128)(2,1)S(1)}, f32[48,128,128]{2,1,0:T(8,128)S(1)}, bf16[48,128,128]{2,1,0:T(8,128)(2,1)S(1)}) custom-call(s32[1,48]{1,0:T(1,128)} %bitcast.1, bf16[48,128,128]{2,1,0:T(8,128)(2,1)} %rhs_h.1, bf16[1,128,128]{2,1,0:T(8,128)(2,1)} %prhs_h.1, bf16[48,128,128]{2,1,0:T(8,128)(2,1)} %linv_h.1, ...), custom_call_target="tpu_custom_call" | custom-call | tf_op jit(solution)/shard_map/pallas_call | solution.py:405
  45.8 0.0 copy-done
  45.8 2.5 %shard_map.105 = (bf16[48,128,128]{2,1,0:T(8,128)(2,1)}, bf16[1,128,128]{2,1,0:T(8,128)(2,1)}) custom-call(s32[48]{0:T(128)S(1)} %copy-done, bf16[256,32,128]{2,1,0:T(8,128)(2,1)S(1)} %get-tuple-element.5.gath, f32[48,128,128]{2,1,0:T(8,128)S(1)} %get-tuple-element.6.ufwd, bf16[48,128,128]{2,1,0:T(8,128)(2,1)S(1)} %get-tuple-element.7.mat), custom_call_target="tpu_custom_call" | custom-call | tf_op jit(solution)/shard_map/pallas_call | solution.py:463
Async XLA Ops:
  0.6 45.2 %copy-start = (s32[48]{0:T(128)S(1)}, s32[48]{0:T(128)}, u32[]{:S(2)}) copy-start(s32[48]{0:T(128)} %po.1) | copy-start | bytes 580

commit v6 on v5

--- a/solution.py
+++ b/solution.py
@@ -209,36 +209,36 @@
 
     order = (2, 1, 3, 0)
     far_first = (3, 2, 1, 0)
+    rows_first = [(t, e) for ts in ((3, 2), (1, 0)) for e in order[:3] for t in ts]
+    rows_first += [(t, 0) for t in far_first]
 
     def row_of(b_):
         return pl.ds(b_ * 8, 8)
 
     waited = False
-    for e in order:
-        for t in far_first:
-            b_ = bx[t][e]
-            for a_ in range(4):
-                for zz in range(2):
-                    v = mine_of(t, b_, a_, zz, flip)
-                    sib[t, b_ * 8 + a_ * 2 + zz] = v.astype(BF)
-            if not waited:
-                pl.semaphore_wait(barrier, len(peers))
-                waited = True
-            rows_ = row_of(b_)
-            send(sib.at[t, rows_], sibr.at[t, rows_], slot("s0", t, e), d_sib)
-
-    for e in order:
-        for t in far_first:
-            b_ = bx[t][e]
-            arrived(sibr.at[t, row_of(b_)], slot("s0", t, e))
-            for d in order[:3]:
-                a_ = ax[t][d]
-                for zz in range(2):
-                    u = b_ * 8 + a_ * 2 + zz
-                    v = mine_of(t, b_, a_, zz, core) + sibr[t, u].astype(F32)
-                    snd[t, u] = v.astype(BF)
-                src = snd.at[t, pl.ds(b_ * 8 + a_ * 2, 2)]
-                send(src, fin.at[t, d - 1, e], slot("f", t, d, e), d_a[t][d])
+    for t, e in rows_first:
+        b_ = bx[t][e]
+        for a_ in range(4):
+            for zz in range(2):
+                v = mine_of(t, b_, a_, zz, flip)
+                sib[t, b_ * 8 + a_ * 2 + zz] = v.astype(BF)
+        if not waited:
+            pl.semaphore_wait(barrier, len(peers))
+            waited = True
+        rows_ = row_of(b_)
+        send(sib.at[t, rows_], sibr.at[t, rows_], slot("s0", t, e), d_sib)
+
+    for t, e in rows_first:
+        b_ = bx[t][e]
+        arrived(sibr.at[t, row_of(b_)], slot("s0", t, e))
+        for d in order[:3]:
+            a_ = ax[t][d]
+            for zz in range(2):
+                u = b_ * 8 + a_ * 2 + zz
+                v = mine_of(t, b_, a_, zz, core) + sibr[t, u].astype(F32)
+                snd[t, u] = v.astype(BF)
+            src = snd.at[t, pl.ds(b_ * 8 + a_ * 2, 2)]
+            send(src, fin.at[t, d - 1, e], slot("f", t, d, e), d_a[t][d])
 
     def at_a(t, e, zz):
         b_, a_ = bx[t][e], ax[t][0]
@@ -247,18 +247,17 @@
             v = v + fin[t, d, e, zz].astype(F32)
         return v
 
-    for e in order:
-        for t in far_first:
-            for d in order[:3]:
-                arrived(fin.at[t, d - 1, e], slot("f", t, d, e))
-            for zz in range(2):
-                v = at_a(t, e, zz)
-                if e == 0:
-                    held[t * 2 + zz] = v
-                else:
-                    snd2[t, e - 1, zz] = v.astype(BF)
-            if e:
-                send(snd2.at[t, e - 1], gin.at[t, e - 1], slot("g", t, e), d_b[t][e])
+    for t, e in rows_first:
+        for d in order[:3]:
+            arrived(fin.at[t, d - 1, e], slot("f", t, d, e))
+        for zz in range(2):
+            v = at_a(t, e, zz)
+            if e == 0:
+                held[t * 2 + zz] = v
+            else:
+                snd2[t, e - 1, zz] = v.astype(BF)
+        if e:
+            send(snd2.at[t, e - 1], gin.at[t, e - 1], slot("g", t, e), d_b[t][e])
 
     for t in far_first:
         for e in order[:3]:

time: 48.4 us -> 48.1 us (level)
  no operation moved by 1% of the time
where the time goes in v6:
time: 48.1 us
  Pallas kernels  47.4 us (99%)
  between operations  0.66 us (1%)
    pallas_call x1, Pallas kernels, on_device(): pl.pallas_call(forward_kernel, out_shape=(jax.ShapeDtypeStruct((256, 32,...  44.9 us
    pallas_call x1, Pallas kernels, on_device(): pl.pallas_call(backward_kernel, out_shape=(jax.ShapeDtypeStruct(child_rhs...  2.47 us

profile of v6, /device:TPU:1, one launch (start us, length us, event | category | flops | bytes accessed | tf_op | source)
XLA Modules:
  0.0 48.1 jit_solution(5281878028511613615)
XLA Ops:
  0.6 0.0 copy-start
  0.6 44.9 %shard_map.104 = (bf16[256,32,128]{2,1,0:T(8,128)(2,1)S(1)}, f32[48,128,128]{2,1,0:T(8,128)S(1)}, bf16[48,128,128]{2,1,0:T(8,128)(2,1)S(1)}) custom-call(s32[1,48]{1,0:T(1,128)} %bitcast.1, bf16[48,128,128]{2,1,0:T(8,128)(2,1)} %rhs_h.1, bf16[1,128,128]{2,1,0:T(8,128)(2,1)} %prhs_h.1, bf16[48,128,128]{2,1,0:T(8,128)(2,1)} %linv_h.1, ...), custom_call_target="tpu_custom_call" | custom-call | tf_op jit(solution)/shard_map/pallas_call | solution.py:404
  45.6 0.0 copy-done
  45.6 2.5 %shard_map.105 = (bf16[48,128,128]{2,1,0:T(8,128)(2,1)}, bf16[1,128,128]{2,1,0:T(8,128)(2,1)}) custom-call(s32[48]{0:T(128)S(1)} %copy-done, bf16[256,32,128]{2,1,0:T(8,128)(2,1)S(1)} %get-tuple-element.5.gath, f32[48,128,128]{2,1,0:T(8,128)S(1)} %get-tuple-element.6.ufwd, bf16[48,128,128]{2,1,0:T(8,128)(2,1)S(1)} %get-tuple-element.7.mat), custom_call_target="tpu_custom_call" | custom-call | tf_op jit(solution)/shard_map/pallas_call | solution.py:462
Async XLA Ops:
  0.6 45.0 %copy-start = (s32[48]{0:T(128)S(1)}, s32[48]{0:T(128)}, u32[]{:S(2)}) copy-start(s32[48]{0:T(128)} %po.1) | copy-start | bytes 580

commit v7 on v6

--- a/solution.py
+++ b/solution.py
@@ -112,7 +112,7 @@
     x_at, y_at = [mod4(x + d) for d in range(4)], [mod4(y + d) for d in range(4)]
     ax, bx = (x_at, y_at) * 2, (y_at, x_at) * 2
 
-    loads, sends, pend = [], [], {}
+    loads = []
 
     def load(src, dst):
         cp = pltpu.make_async_copy(src, dst, load_sem.at[len(loads)])
@@ -182,30 +182,27 @@
         last_ = tab[0, 64 + y_ * 16 + zs[NEAR[t * 2 + zz]] * 2 + core_]
         return run[last_, pl.ds(row, 32), :]
 
-    def remote(src, dst, slot, dev_):
+    stages = ("s0", "f", "g", "z", "bz", "bb", "ba", "o")
+    slots = {}
+
+    def slot(*key):
+        return slots.setdefault(key, len(slots))
+
+    def remote(src, dst, sent, got, dev_):
         return pltpu.make_async_remote_copy(
             src_ref=src,
             dst_ref=dst,
-            send_sem=send_sem.at[slot],
-            recv_sem=recv_sem.at[slot],
+            send_sem=send_sem.at[sent],
+            recv_sem=recv_sem.at[got],
             device_id=dev_,
             device_id_type=MESH,
         )
 
-    def send(src, dst, slot, dev_):
-        cp = remote(src, dst, slot, dev_)
-        cp.start()
-        sends.append(cp)
-        pend[slot] = src
-
-    def arrived(dst, slot):
-        remote(dst, dst, slot, d_sib).wait_recv()
-        pend.pop(slot)
-
-    slots = {}
-
-    def slot(*key):
-        return slots.setdefault(key, len(slots))
+    def send(src, dst, dev_, stage, *key):
+        remote(src, dst, stages.index(stage), slot(stage, *key), dev_).start()
+
+    def arrived(dst, *key):
+        remote(dst, dst, 0, slot(*key), d_sib).wait_recv()
 
     order = (2, 1, 3, 0)
     far_first = (3, 2, 1, 0)
@@ -226,11 +223,11 @@
             pl.semaphore_wait(barrier, len(peers))
             waited = True
         rows_ = row_of(b_)
-        send(sib.at[t, rows_], sibr.at[t, rows_], slot("s0", t, e), d_sib)
+        send(sib.at[t, rows_], sibr.at[t, rows_], d_sib, "s0", t, e)
 
     for t, e in rows_first:
         b_ = bx[t][e]
-        arrived(sibr.at[t, row_of(b_)], slot("s0", t, e))
+        arrived(sibr.at[t, row_of(b_)], "s0", t, e)
         for d in order[:3]:
             a_ = ax[t][d]
             for zz in range(2):
@@ -238,18 +235,17 @@
                 v = mine_of(t, b_, a_, zz, core) + sibr[t, u].astype(F32)
                 snd[t, u] = v.astype(BF)
             src = snd.at[t, pl.ds(b_ * 8 + a_ * 2, 2)]
-            send(src, fin.at[t, d - 1, e], slot("f", t, d, e), d_a[t][d])
+            send(src, fin.at[t, e, d - 1], d_a[t][d], "f", t, e)
 
     def at_a(t, e, zz):
         b_, a_ = bx[t][e], ax[t][0]
         v = mine_of(t, b_, a_, zz, core) + sibr[t, b_ * 8 + a_ * 2 + zz].astype(F32)
         for d in range(3):
-            v = v + fin[t, d, e, zz].astype(F32)
+            v = v + fin[t, e, d, zz].astype(F32)
         return v
 
     for t, e in rows_first:
-        for d in order[:3]:
-            arrived(fin.at[t, d - 1, e], slot("f", t, d, e))
+        arrived(fin.at[t, e], "f", t, e)
         for zz in range(2):
             v = at_a(t, e, zz)
             if e == 0:
@@ -257,11 +253,10 @@
             else:
                 snd2[t, e - 1, zz] = v.astype(BF)
         if e:
-            send(snd2.at[t, e - 1], gin.at[t, e - 1], slot("g", t, e), d_b[t][e])
+            send(snd2.at[t, e - 1], gin.at[t, e - 1], d_b[t][e], "g", t)
 
     for t in far_first:
-        for e in order[:3]:
-            arrived(gin.at[t, e - 1], slot("g", t, e))
+        arrived(gin.at[t], "g", t)
         for zz in (1, 0):
             pos = t * 2 + zz
             v = held[pos]
@@ -272,7 +267,7 @@
                 continue
             d = NEAR[pos]
             zr_out[d - 1] = v.astype(BF)
-            send(zr_out.at[d - 1], zr.at[d - 1], slot("z", d), d_z[d])
+            send(zr_out.at[d - 1], zr.at[d - 1], d_z[d], "z")
     held[0] = total
 
     for cp in parent_loads:
@@ -291,8 +286,8 @@
     loop(NCH // 4, prepare)
 
     total = held[0]
+    arrived(zr, "z")
     for d in range(1, 8):
-        arrived(zr.at[d - 1], slot("z", d))
         total = total + zr[d - 1].astype(F32)
 
     res = (prt[pl.ds(pl.multiple_of(x * 32, 32), 32), :] - total).astype(BF)
@@ -306,38 +301,36 @@
     gath[unit(0)] = sol[...]
 
     for d in (4, 3, 5, 2, 6, 1, 7):
-        dst = gath.at[unit(NEAR.index(8 - d))]
-        send(sol, dst, slot("bz", d), d_z[d])
-
-    def share(ref_slice, slot_, dev_):
-        send(gath.at[ref_slice], gath.at[ref_slice], slot_, dev_)
-
-    def piece(t, e, d, core_=core):
-        return pl.ds((core_ * 4 + t) * 32 + bx[t][e] * 8 + ax[t][d] * 2, 2)
-
-    def whole_row(t, e, core_=core):
-        return pl.ds((core_ * 4 + t) * 32 + bx[t][e] * 8, 8)
+        pos = NEAR.index(8 - d)
+        send(sol, gath.at[unit(pos)], d_z[d], "bz", pos // 2)
+
+    def share(ref_slice, dev_, *key):
+        send(gath.at[ref_slice], gath.at[ref_slice], dev_, *key)
+
+    def piece(t, e, d):
+        return pl.ds((core * 4 + t) * 32 + bx[t][e] * 8 + ax[t][d] * 2, 2)
+
+    def whole_row(t, e, n=8):
+        return pl.ds((core * 4 + t) * 32 + bx[t][e] * 8, n)
 
     def along_a(t, e):
         for d in order[:3]:
-            share(piece(t, e, 0), slot("ba", t, e, d), d_a[t][d])
+            share(piece(t, e, 0), d_a[t][d], "ba", t, e)
 
     def along_b(t):
-        for pos in (t * 2, t * 2 + 1):
-            if pos:
-                arrived(gath.at[unit(pos)], slot("bz", 8 - NEAR[pos]))
+        new = pl.ds(unit(0) + 1, 1) if t == 0 else piece(t, 0, 0)
+        arrived(gath.at[new], "bz", t)
         for e in order[:3]:
-            share(piece(t, 0, 0), slot("bb", t, e), d_b[t][e])
+            share(piece(t, 0, 0), d_b[t][e], "bb", t, e)
         along_a(t, 0)
 
     def along_row(t, e):
-        arrived(gath.at[piece(t, e, 0)], slot("bb", t, 4 - e))
+        arrived(gath.at[piece(t, e, 0)], "bb", t, 4 - e)
         along_a(t, e)
 
     def across(t, e):
-        for d in (1, 3, 2):
-            arrived(gath.at[piece(t, e, d)], slot("ba", t, e, 4 - d))
-        share(whole_row(t, e), slot("o", t, e), d_sib)
+        arrived(gath.at[whole_row(t, e, 6)], "ba", t, e)
+        share(whole_row(t, e), d_sib, "o")
 
     for t in PARTS:
         along_b(t)
@@ -355,11 +348,10 @@
     for e in (0, 1, 3, 2):
         for t in (2, 3):
             across(t, e)
-    for t in PARTS:
-        for e in (0, 1, 3, 2):
-            arrived(gath.at[whole_row(t, e, flip)], slot("o", t, e))
-    for cp in sends:
-        cp.wait_send()
+    arrived(gath.at[pl.ds(flip * 128, 128)], "o")
+    most = snd.at[pl.ds(0, 3)]
+    for i, sent in enumerate((sib, most, snd2, zr_out, zr_out, snd2, most, sib)):
+        remote(sent, sent, i, 0, d_sib).wait_send()
 
 
 def backward_kernel(po, gath, ufwd, mat, out_h, psol_h, out, psol, sem):
@@ -427,7 +419,7 @@
             units(4, 32),
             units(4, 32),
             units(4, 32),
-            units(4, 3, 4, 2),
+            units(4, 4, 3, 2),
             units(4, 3, 2),
             units(4, 3, 2),
             pltpu.VMEM((8, 32, 128), F32),
@@ -437,8 +429,8 @@
             pltpu.VMEM((128, 128), F32),
             pltpu.SemaphoreType.DMA((3 * CHUNKS + 9,)),
             pltpu.SemaphoreType.DMA((1,)),
-            pltpu.SemaphoreType.DMA((166,)),
-            pltpu.SemaphoreType.DMA((166,)),
+            pltpu.SemaphoreType.DMA((8,)),
+            pltpu.SemaphoreType.DMA((70,)),
         ],
         compiler_params=pltpu.CompilerParams(
             collective_id=0, has_side_effects=True, vmem_limit_bytes=40 * 2**20

time: 48.1 us -> 45.6 us (0.948)
  Pallas kernels: 47.4 us -> 44.9 us
    pallas_call x1, Pallas kernels: 44.9 us -> 42.4 us  [on_device(): pl.pallas_call(forward_kernel, out_shape=(jax.ShapeDtypeStruct((256, 32,...]
where the time goes in v7:
time: 45.6 us; the launch traced here: 45.5 us
  Pallas kernels  44.9 us (98%)
  between operations  0.66 us (1%)
    pallas_call x1, Pallas kernels, on_device(): pl.pallas_call(forward_kernel, out_shape=(jax.ShapeDtypeStruct((256, 32,...  42.4 us
    pallas_call x1, Pallas kernels, on_device(): pl.pallas_call(backward_kernel, out_shape=(jax.ShapeDtypeStruct(child_rhs...  2.47 us

profile of v7, /device:TPU:1, one launch (start us, length us, event | category | flops | bytes accessed | tf_op | source)
XLA Modules:
  0.0 45.5 jit_solution(1119869611360217980)
XLA Ops:
  0.6 0.0 copy-start
  0.6 42.4 %shard_map.104 = (bf16[256,32,128]{2,1,0:T(8,128)(2,1)S(1)}, f32[48,128,128]{2,1,0:T(8,128)S(1)}, bf16[48,128,128]{2,1,0:T(8,128)(2,1)S(1)}) custom-call(s32[1,48]{1,0:T(1,128)} %bitcast.1, bf16[48,128,128]{2,1,0:T(8,128)(2,1)} %rhs_h.1, bf16[1,128,128]{2,1,0:T(8,128)(2,1)} %prhs_h.1, bf16[48,128,128]{2,1,0:T(8,128)(2,1)} %linv_h.1, ...), custom_call_target="tpu_custom_call" | custom-call | tf_op jit(solution)/shard_map/pallas_call | solution.py:396
  43.0 0.0 copy-done
  43.0 2.5 %shard_map.105 = (bf16[48,128,128]{2,1,0:T(8,128)(2,1)}, bf16[1,128,128]{2,1,0:T(8,128)(2,1)}) custom-call(s32[48]{0:T(128)S(1)} %copy-done, bf16[256,32,128]{2,1,0:T(8,128)(2,1)S(1)} %get-tuple-element.5.gath, f32[48,128,128]{2,1,0:T(8,128)S(1)} %get-tuple-element.6.ufwd, bf16[48,128,128]{2,1,0:T(8,128)(2,1)S(1)} %get-tuple-element.7.mat), custom_call_target="tpu_custom_call" | custom-call | tf_op jit(solution)/shard_map/pallas_call | solution.py:454
Async XLA Ops:
  0.6 42.4 %copy-start = (s32[48]{0:T(128)S(1)}, s32[48]{0:T(128)}, u32[]{:S(2)}) copy-start(s32[48]{0:T(128)} %po.1) | copy-start | bytes 580

commit v8 on v7

--- a/solution.py
+++ b/solution.py
@@ -112,26 +112,35 @@
     x_at, y_at = [mod4(x + d) for d in range(4)], [mod4(y + d) for d in range(4)]
     ax, bx = (x_at, y_at) * 2, (y_at, x_at) * 2
 
-    loads = []
-
-    def load(src, dst):
-        cp = pltpu.make_async_copy(src, dst, load_sem.at[len(loads)])
-        cp.start()
-        loads.append(cp)
-        return cp
+    group = [0]
+
+    def load(*pairs, whole=None):
+        sem = load_sem.at[group[0]]
+        group[0] += 1
+        for src, dst in pairs:
+            pltpu.make_async_copy(src, dst, sem).start()
+        return pltpu.make_async_copy(*(whole or pairs[0]), sem)
 
     starts = [0, 4] + list(range(8, NCH + 1, GRP))
     spans = list(zip(starts[:-1], starts[1:], strict=True))
 
     def load_span(lo, hi):
-        part = pl.ds(lo, hi - lo)
+        part, size = pl.ds(lo, hi - lo), pl.ds(0, 3 * (hi - lo))
         pairs = ((linv_h, linv), (rhs_h, rhs), (loff_h, loff))
-        return [load(src.at[part], dst.at[part]) for src, dst in pairs]
-
-    po_load = load(po_h, pov)
+        return load(
+            *[(src.at[part], dst.at[part]) for src, dst in pairs],
+            whole=(linv_h.at[size], linv.at[size]),
+        )
+
+    po_load = load((po_h, pov))
     span_loads = [load_span(*span) for span in spans]
-    upper_loads = [load(uinv_h, uinv), load(uoff_h, uoff)]
-    parent_loads = [load(prhs_h, prhs), load(plinv_h, plinv), load(puinv_h, puinv)]
+    upper_loads = [load((uinv_h, uinv)), load((uoff_h, uoff))]
+    parent_load = load(
+        (prhs_h, prhs),
+        (plinv_h, plinv),
+        (puinv_h, puinv),
+        whole=(linv_h.at[pl.ds(0, 3)], linv.at[pl.ds(0, 3)]),
+    )
 
     barrier = pltpu.get_barrier_semaphore()
     peers = [d_sib] + d_x[1:] + d_y[1:] + d_z[1:]
@@ -158,8 +167,7 @@
 
     tab_copy = table()
     for k, (lo, hi) in enumerate(spans):
-        for cp in span_loads[k]:
-            cp.wait()
+        span_loads[k].wait()
         terms = []
         for c in range(lo, hi):
             f = mm(linv[c], rhs[c]).astype(BF)
@@ -270,8 +278,7 @@
             send(zr_out.at[d - 1], zr.at[d - 1], d_z[d], "z")
     held[0] = total
 
-    for cp in parent_loads:
-        cp.wait()
+    parent_load.wait()
     prt[...] = prhs[0].astype(F32).T
     for cp in upper_loads:
         cp.wait()
@@ -321,12 +328,15 @@
         new = pl.ds(unit(0) + 1, 1) if t == 0 else piece(t, 0, 0)
         arrived(gath.at[new], "bz", t)
         for e in order[:3]:
-            share(piece(t, 0, 0), d_b[t][e], "bb", t, e)
+            share(piece(t, 0, 0), d_b[t][e], "bb", t, e == 2)
         along_a(t, 0)
 
-    def along_row(t, e):
-        arrived(gath.at[piece(t, e, 0)], "bb", t, 4 - e)
-        along_a(t, e)
+    def along_rows(t):
+        arrived(gath.at[whole_row(t, 0, 4)], "bb", t, False)
+        along_a(t, 1)
+        along_a(t, 3)
+        arrived(gath.at[piece(t, 2, 0)], "bb", t, True)
+        along_a(t, 2)
 
     def across(t, e):
         arrived(gath.at[whole_row(t, e, 6)], "ba", t, e)
@@ -335,13 +345,11 @@
     for t in PARTS:
         along_b(t)
     for t in (0, 1):
-        for e in (1, 3, 2):
-            along_row(t, e)
+        along_rows(t)
     for t in (0, 1):
         across(t, 0)
     for t in (2, 3):
-        for e in (1, 3, 2):
-            along_row(t, e)
+        along_rows(t)
     for t in (0, 1):
         for e in (1, 3, 2):
             across(t, e)
@@ -358,22 +366,15 @@
     col = lax.axis_index("col")
     z = lax.rem(lax.div(col, 2), 8)
     psol[0] = parent_of_units(gath, col, z).T
-    copies = []
-
-    def put(src, dst):
-        cp = pltpu.make_async_copy(src, dst, sem.at[len(copies)])
-        cp.start()
-        copies.append(cp)
-
-    put(psol, psol_h)
+    pltpu.make_async_copy(psol, psol_h, sem.at[0]).start()
     for k in range(CHUNKS):
         for c in range(k * GRP, (k + 1) * GRP):
             s = parent_of_units(gath, po[c], z)
             out[c] = (ufwd[c] - mm_nt(mat[c], s)).astype(BF)
         part = pl.ds(k * GRP, GRP)
-        put(out.at[part], out_h.at[part])
-    for cp in copies:
-        cp.wait()
+        pltpu.make_async_copy(out.at[part], out_h.at[part], sem.at[1]).start()
+    pltpu.make_async_copy(psol, psol_h, sem.at[0]).wait()
+    pltpu.make_async_copy(out, out_h, sem.at[1]).wait()
 
 
 def on_device(
@@ -427,10 +428,10 @@
             units(7),
             units(),
             pltpu.VMEM((128, 128), F32),
-            pltpu.SemaphoreType.DMA((3 * CHUNKS + 9,)),
+            pltpu.SemaphoreType.DMA((CHUNKS + 5,)),
             pltpu.SemaphoreType.DMA((1,)),
             pltpu.SemaphoreType.DMA((8,)),
-            pltpu.SemaphoreType.DMA((70,)),
+            pltpu.SemaphoreType.DMA((66,)),
         ],
         compiler_params=pltpu.CompilerParams(
             collective_id=0, has_side_effects=True, vmem_limit_bytes=40 * 2**20
@@ -459,7 +460,7 @@
         ),
         in_specs=[smem, vmem, vmem, vmem],
         out_specs=(hbm, hbm),
-        scratch_shapes=[mats(), one(), pltpu.SemaphoreType.DMA((CHUNKS + 1,))],
+        scratch_shapes=[mats(), one(), pltpu.SemaphoreType.DMA((2,))],
         compiler_params=pltpu.CompilerParams(vmem_limit_bytes=16 * 2**20),
     )(parent_of, gath, ufwd, mat)
 

time: 45.6 us -> 45.3 us (level)
  no operation moved by 1% of the time
where the time goes in v8:
time: 45.3 us; the launch traced here: 45.2 us
  Pallas kernels  44.6 us (98%)
  between operations  0.66 us (1%)
    pallas_call x1, Pallas kernels, on_device(): pl.pallas_call(forward_kernel, out_shape=(jax.ShapeDtypeStruct((256, 32,...  42.2 us
    pallas_call x1, Pallas kernels, on_device(): pl.pallas_call(backward_kernel, out_shape=(jax.ShapeDtypeStruct(child_rhs...  2.42 us

profile of v8, /device:TPU:1, one launch (start us, length us, event | category | flops | bytes accessed | tf_op | source)
XLA Modules:
  0.0 45.2 jit_solution(16507513993477211320)
XLA Ops:
  0.6 0.0 copy-start
  0.6 42.2 %shard_map.104 = (bf16[256,32,128]{2,1,0:T(8,128)(2,1)S(1)}, f32[48,128,128]{2,1,0:T(8,128)S(1)}, bf16[48,128,128]{2,1,0:T(8,128)(2,1)S(1)}) custom-call(s32[1,48]{1,0:T(1,128)} %bitcast.1, bf16[48,128,128]{2,1,0:T(8,128)(2,1)} %rhs_h.1, bf16[1,128,128]{2,1,0:T(8,128)(2,1)} %prhs_h.1, bf16[48,128,128]{2,1,0:T(8,128)(2,1)} %linv_h.1, ...), custom_call_target="tpu_custom_call" | custom-call | tf_op jit(solution)/shard_map/pallas_call | solution.py:397
  42.8 0.0 copy-done
  42.8 2.4 %shard_map.105 = (bf16[48,128,128]{2,1,0:T(8,128)(2,1)}, bf16[1,128,128]{2,1,0:T(8,128)(2,1)}) custom-call(s32[48]{0:T(128)S(1)} %copy-done, bf16[256,32,128]{2,1,0:T(8,128)(2,1)S(1)} %get-tuple-element.5.gath, f32[48,128,128]{2,1,0:T(8,128)S(1)} %get-tuple-element.6.ufwd, bf16[48,128,128]{2,1,0:T(8,128)(2,1)S(1)} %get-tuple-element.7.mat), custom_call_target="tpu_custom_call" | custom-call | tf_op jit(solution)/shard_map/pallas_call | solution.py:455
Async XLA Ops:
  0.6 42.2 %copy-start = (s32[48]{0:T(128)S(1)}, s32[48]{0:T(128)}, u32[]{:S(2)}) copy-start(s32[48]{0:T(128)} %po.1) | copy-start | bytes 580

commit v9 on v8

--- a/solution.py
+++ b/solution.py
@@ -109,6 +109,9 @@
     zs = [lax.rem(z + d, 8) for d in range(8)]
     d_z = [dev(x, y, zs[d], core) for d in range(8)]
     d_a, d_b = (d_x, d_y) * 2, (d_y, d_x) * 2
+    o_x = [dev(mod4(x + d), y, z, flip) for d in range(4)]
+    o_y = [dev(x, mod4(y + d), z, flip) for d in range(4)]
+    o_a = (o_x, o_y) * 2
     x_at, y_at = [mod4(x + d) for d in range(4)], [mod4(y + d) for d in range(4)]
     ax, bx = (x_at, y_at) * 2, (y_at, x_at) * 2
 
@@ -143,7 +146,7 @@
     )
 
     barrier = pltpu.get_barrier_semaphore()
-    peers = [d_sib] + d_x[1:] + d_y[1:] + d_z[1:]
+    peers = o_x + o_y[1:] + d_x[1:] + d_y[1:] + d_z[1:]
     for peer in peers:
         pl.semaphore_signal(barrier, inc=1, device_id=peer, device_id_type=MESH)
 
@@ -337,9 +340,14 @@
         along_a(t, 3)
         arrived(gath.at[piece(t, 2, 0)], "bb", t, True)
         along_a(t, 2)
+        if t > 1:
+            for d in (2, 1, 3, 0):
+                share(piece(t, 2, 0), o_a[t][d], "o")
 
     def across(t, e):
         arrived(gath.at[whole_row(t, e, 6)], "ba", t, e)
+        if (t > 1) and (e == 2):
+            return
         share(whole_row(t, e), d_sib, "o")
 
     for t in PARTS:

time: 45.3 us -> 45.2 us (level)
  no operation moved by 1% of the time
where the time goes in v9:
time: 45.2 us; the launch traced here: 45.3 us
  Pallas kernels  44.6 us (99%)
  between operations  0.66 us (1%)
    pallas_call x1, Pallas kernels, on_device(): pl.pallas_call(forward_kernel, out_shape=(jax.ShapeDtypeStruct((256, 32,...  42.2 us
    pallas_call x1, Pallas kernels, on_device(): pl.pallas_call(backward_kernel, out_shape=(jax.ShapeDtypeStruct(child_rhs...  2.42 us

profile of v9, /device:TPU:1, one launch (start us, length us, event | category | flops | bytes accessed | tf_op | source)
XLA Modules:
  0.0 45.3 jit_solution(8592932304336602633)
XLA Ops:
  0.6 0.0 copy-start
  0.6 42.2 %shard_map.104 = (bf16[256,32,128]{2,1,0:T(8,128)(2,1)S(1)}, f32[48,128,128]{2,1,0:T(8,128)S(1)}, bf16[48,128,128]{2,1,0:T(8,128)(2,1)S(1)}) custom-call(s32[1,48]{1,0:T(1,128)} %bitcast.1, bf16[48,128,128]{2,1,0:T(8,128)(2,1)} %rhs_h.1, bf16[1,128,128]{2,1,0:T(8,128)(2,1)} %prhs_h.1, bf16[48,128,128]{2,1,0:T(8,128)(2,1)} %linv_h.1, ...), custom_call_target="tpu_custom_call" | custom-call | tf_op jit(solution)/shard_map/pallas_call | solution.py:405
  42.8 0.0 copy-done
  42.9 2.4 %shard_map.105 = (bf16[48,128,128]{2,1,0:T(8,128)(2,1)}, bf16[1,128,128]{2,1,0:T(8,128)(2,1)}) custom-call(s32[48]{0:T(128)S(1)} %copy-done, bf16[256,32,128]{2,1,0:T(8,128)(2,1)S(1)} %get-tuple-element.5.gath, f32[48,128,128]{2,1,0:T(8,128)S(1)} %get-tuple-element.6.ufwd, bf16[48,128,128]{2,1,0:T(8,128)(2,1)S(1)} %get-tuple-element.7.mat), custom_call_target="tpu_custom_call" | custom-call | tf_op jit(solution)/shard_map/pallas_call | solution.py:463
Async XLA Ops:
  0.6 42.2 %copy-start = (s32[48]{0:T(128)S(1)}, s32[48]{0:T(128)}, u32[]{:S(2)}) copy-start(s32[48]{0:T(128)} %po.1) | copy-start | bytes 580
